TPU v7x, 256 devices: a whole 4x4x8 slice. The times are simulated.
256 devices in a mesh: section: 4 (over x), row: 8 (over z), col: 8 (over y, core).
Axes of the slice: x: 4, y: 4, z: 8, core: 2. Of those that a mesh axis runs over, the one named last changes fastest.
Arguments:
- statistic: float32 [8192, 2048], P(('section', 'row'), 'col'), parts along dimension 0, as said below
- gradient: bfloat16 [8192, 28672], P('section', ('row', 'col')), parts along dimension 0, may hold values from -6 to 6
Outputs:
- next_m: float32 [8192, 2048], P(('section', 'row'), 'col'), parts along dimension 0
- preconditioned: bfloat16 [8192, 28672], P('section', ('row', 'col')), parts along dimension 0
- next_diag: float32 [8192], P(('section', 'row')), parts along dimension 0
There are 4 independent parts, one for each index of `section`. A program takes and returns all parts, laid end to end along the dimension named above; each array names one. Nothing has to cross between parts.
Inputs may be any that keep to these rules, and one draw needn't show every extreme that they name: `statistic`: symmetric and positive definite.
All inputs are finite; a program needn't handle non-finite values.
Results may differ from a plain program's by a relative error of at most 0.0052.
Values may be sent and summed in bfloat16 or wider, within the bound.
No kernel may reach another device: no remote copies, remote signals or barrier semaphores. Data moves between devices by JAX's collectives and lax.ppermute only.
A program may use at most 64 MiB of HBM per device.

v0:
```python
import jax
import jax.numpy as jnp
from jax import lax
from jax.sharding import PartitionSpec as P

BLOCK = 2048


def copy_for_each(x, axis):
    copies = jnp.broadcast_to(x, (lax.axis_size(axis), *x.shape))
    return lax.all_to_all(copies, axis, split_axis=0, concat_axis=0, tiled=True)


def taken_together(x, axis):
    return copy_for_each(x, axis).sum(axis=0)


def laid_out(parts, dim):
    parts = jnp.moveaxis(parts, 0, dim)
    shape = parts.shape
    return parts.reshape(*shape[:dim], shape[dim] * shape[dim + 1], *shape[dim + 2 :])


def gathered_copies(x, axis, dim):
    return laid_out(copy_for_each(x, axis), dim)


def fold_with(panel, piece):
    return jnp.dot(
        panel, piece, precision=lax.Precision.HIGHEST, preferred_element_type=jnp.float32
    )


def local(statistic, gradient):
    highest = lax.Precision.HIGHEST
    rows_here, cols_here = statistic.shape
    total = taken_together(jnp.sum(statistic * statistic), ("row", "col"))
    scale4 = jnp.sqrt(BLOCK * (total / (BLOCK * BLOCK) + 1e-06))
    row_ids = lax.axis_index("row") * rows_here + jnp.arange(rows_here, dtype=jnp.int32)
    col_start = lax.axis_index("col") * cols_here
    col_ids = col_start + jnp.arange(cols_here, dtype=jnp.int32)
    ident = (row_ids[:, None] == col_ids[None, :]).astype(jnp.float32)
    m_start = statistic / scale4
    t_block = (5.0 * ident - m_start) / 4.0
    t_rows = gathered_copies(t_block, "col", 1)
    m_cols = lax.all_gather(m_start, "row", axis=0, tiled=True)
    every_row = jnp.arange(BLOCK, dtype=jnp.int32)
    ident_cols = (every_row[:, None] == col_ids[None, :]).astype(jnp.float32)
    t_cols = (5.0 * ident_cols - m_cols) / 4.0
    square = jnp.dot(t_rows, t_cols, precision=highest, preferred_element_type=jnp.float32)
    square_rows = gathered_copies(square, "col", 1)
    third = jnp.dot(square_rows, m_cols, precision=highest, preferred_element_type=jnp.float32)
    full_block = fold_with(square_rows, gathered_copies(third, "row", 0))
    next_m = full_block * (1.0 - ident)
    square_own = lax.dynamic_slice_in_dim(square_rows, col_start, cols_here, 1)
    partial_diag = jnp.sum(square_own * third, axis=1)
    next_diag = taken_together(partial_diag, "col")
    fourth_root = jnp.sqrt(jnp.sqrt(scale4))
    x_block = (t_block / fourth_root).astype(jnp.bfloat16)
    spread = lax.all_gather(x_block, ("row", "col"), axis=1, tiled=True)
    grid_rows = lax.axis_size("row")
    grid_cols = lax.axis_size("col")
    arranged = spread.reshape(rows_here, grid_rows, grid_cols, cols_here)
    grad_split = gradient.reshape(grid_cols, cols_here, gradient.shape[1])
    product = jnp.einsum("aijc,jcf->iaf", arranged, grad_split, preferred_element_type=jnp.float32)
    preconditioned = product.reshape(BLOCK, gradient.shape[1]).astype(jnp.bfloat16)
    return (next_m, preconditioned, next_diag)


def solution(mesh):
    return jax.shard_map(
        local,
        mesh=mesh,
        in_specs=(P(("section", "row"), "col"), P("section", ("row", "col"))),
        out_specs=(
            P(("section", "row"), "col"),
            P("section", ("row", "col")),
            P(("section", "row")),
        ),
        check_vma=False,
    )
```

profile of v0, /device:TPU:1, one launch (start us, length us, event | category | flops | bytes accessed | tf_op | source)
XLA Modules:
  0.0 232.3 jit_solution(10723034201758817367)
XLA Ops:
  7.2 1.6 multiply_reduce_fusion.1
  8.8 1.3 broadcast_in_dim.19
  10.1 13.1 %all-to-all-start = ((f32[64,1,1]{2,1,0:T(1,128)}), f32[64,1,1]{2,1,0:T(1,128)S(1)}, u32[]{:S(2)}, u32[]{:S(2)}) async-start(f32[64,1,1]{2,1,0:T(1,128)} %broadcast_in_dim.19), calls=%async_computation | async-start | bytes 65536 | tf_op jit(solution)/shard_map/all_to_all | solution.py:11
  23.2 0.0 all-gather.3.cloned.1.call-start
  23.3 9.3 %all-to-all-done = f32[64,1,1]{2,1,0:T(1,128)S(1)} async-done(((f32[64,1,1]{2,1,0:T(1,128)}), f32[64,1,1]{2,1,0:T(1,128)S(1)}, u32[]{:S(2)}, u32[]{:S(2)}) %all-to-all-start) | async-done | bytes 288 | tf_op jit(solution)/shard_map/all_to_all | solution.py:11
  32.5 0.7 reduce_sum.37
  34.0 1.7 divide_convert_fusion
  35.7 0.0 all-gather.3.cloned.1.call-update
  35.8 0.0 all-gather.5.cloned.1.call-start
  35.8 0.7 all-gather.5.cloned.1.call-update
  36.5 0.1 copy.22
  36.6 0.2 broadcast_in_dim.20
  36.8 29.3 %all_to_all.27 = f32[8,256,256]{1,2,0:T(8,128)S(1)} all-to-all(f32[8,256,256]{1,2,0:T(8,128)S(1)} %broadcast_in_dim.20), channel_id=1, replica_groups=mesh['section'=4,'row'=8,'col'=8] {'col'}, dimensions={0} | all-to-all | bytes 4194304 | tf_op jit(solution)/shard_map/all_to_all | solution.py:11
  66.2 1.0 all-gather.3.cloned.1.call-done
  67.2 5.2 %fusion.2 = f32[256,256]{1,0:T(8,128)S(1)} fusion(f32[256,2048]{0,1:T(8,128)S(1)} %bitcast.39, f32[2048,256]{1,0:T(8,128)} %all-gather.3.cloned.1.call-done, s32[256]{0:T(256)S(1)} %get-tuple-element.8), kind=kOutput, calls=%fused_computation.3 | convolution fusion | flops 1612709888 | bytes 4457472 | tf_op jit(solution)/shard_map/dot_general | solution.py:50
  72.3 1.5 broadcast_in_dim.21
  73.9 9.3 %all-to-all-start.2 = ((f32[8,256,256]{2,1,0:T(8,128)}), f32[8,256,256]{2,1,0:T(8,128)S(1)}, u32[]{:S(2)}, u32[]{:S(2)}) async-start(f32[8,256,256]{2,1,0:T(8,128)} %broadcast_in_dim.21), calls=%async_computation.2 | async-start | bytes 4194304 | tf_op jit(solution)/shard_map/all_to_all | solution.py:11
  83.1 28.3 %all-to-all-done.2 = f32[8,256,256]{2,1,0:T(8,128)S(1)} async-done(((f32[8,256,256]{2,1,0:T(8,128)}), f32[8,256,256]{2,1,0:T(8,128)S(1)}, u32[]{:S(2)}, u32[]{:S(2)}) %all-to-all-start.2) | async-done | bytes 2097184 | tf_op jit(solution)/shard_map/all_to_all | solution.py:11
  111.4 1.8 copy.23
  113.3 5.7 %multiply_reduce_fusion = (f32[256]{0:T(256)S(1)}, f32[256,256]{0,1:T(8,128)S(1)}) fusion(f32[256,2048]{0,1:T(8,128)} %bitcast.42, s32[]{:T(128)S(6)} %select_n.3, f32[2048,256]{1,0:T(8,128)} %all-gather.3.cloned.1.call-done), kind=kOutput, calls=%fused_computation.22 | convolution fusion | flops 1610743552 | bytes 4719620 | tf_op jit(solution)/shard_map/dot_general | solution.py:52
  119.0 0.6 broadcast_in_dim.23
  119.6 4.2 %all-to-all-start.4 = ((f32[8,1,256]{2,1,0:T(1,128)}), f32[8,1,256]{2,1,0:T(1,128)S(1)}, u32[]{:S(2)}, u32[]{:S(2)}) async-start(f32[8,1,256]{2,1,0:T(1,128)} %broadcast_in_dim.23), calls=%async_computation.4 | async-start | bytes 16384 | tf_op jit(solution)/shard_map/all_to_all | solution.py:11
  123.8 0.1 copy.24
  123.9 4.8 %all-to-all-done.4 = f32[8,1,256]{2,1,0:T(1,128)S(1)} async-done(((f32[8,1,256]{2,1,0:T(1,128)}), f32[8,1,256]{2,1,0:T(1,128)S(1)}, u32[]{:S(2)}, u32[]{:S(2)}) %all-to-all-start.4) | async-done | bytes 8224 | tf_op jit(solution)/shard_map/all_to_all | solution.py:11
  128.7 1.5 broadcast_in_dim.22
  130.2 4.6 %all-to-all-start.3 = ((f32[8,256,256]{2,1,0:T(8,128)}), f32[8,256,256]{2,1,0:T(8,128)}, u32[]{:S(2)}, u32[]{:S(2)}) async-start(f32[8,256,256]{2,1,0:T(8,128)} %broadcast_in_dim.22), calls=%async_computation.3 | async-start | bytes 4194304 | tf_op jit(solution)/shard_map/all_to_all | solution.py:11
  134.7 0.6 reduce_sum.39
  135.3 61.1 %all-to-all-done.3 = f32[8,256,256]{2,1,0:T(8,128)} async-done(((f32[8,256,256]{2,1,0:T(8,128)}), f32[8,256,256]{2,1,0:T(8,128)}, u32[]{:S(2)}, u32[]{:S(2)}) %all-to-all-start.3) | async-done | bytes 2097184 | tf_op jit(solution)/shard_map/all_to_all | solution.py:11
  196.4 4.2 %fusion.12 = f32[256,256]{1,0:T(8,128)} fusion(f32[8,256,256]{2,1,0:T(8,128)} %all-to-all-done.3, s32[256]{0:T(256)S(1)} %get-tuple-element.8, s32[256]{0:T(256)S(1)} %get-tuple-element.9, f32[8,256,256]{2,1,0:T(8,128)S(1)} %all-to-all-done.2), kind=kOutput, calls=%fused_computation.12 | convolution fusion | flops 1610874880 | bytes 4458496 | tf_op jit(solution)/shard_map/dot_general | solution.py:29
  200.6 0.0 all-gather.5.cloned.1.call-done
  200.6 0.0 copy-start
  200.6 9.5 %copy.34 = bf16[32,8,64,256]{3,2,1,0:T(8,128)(2,1)} copy(bf16[32,8,64,256]{3,1,2,0:T(8,128)(2,1)} %bitcast.40) | data formatting | bytes 16777216
  210.1 0.0 copy-done
  210.1 13.9 %fusion.9 = bf16[8,56,8,256]{3,2,1,0:T(8,128)(2,1)S(1)} fusion(bf16[56,8,8,256]{3,2,1,0:T(8,128)(2,1)S(1)} %bitcast.44, bf16[256,8,8,256]{3,2,1,0:T(8,128)(2,1)} %bitcast.41), kind=kOutput, calls=%fused_computation.10 | convolution fusion | flops 3759013888 | bytes 12058624 | tf_op jit(solution)/shard_map/aijc,jcf->iaf/dot_general | solution.py:65
  224.0 1.5 copy.33
  (1 shorter events, 0.0 us)
Async XLA Ops:
  10.1 22.5 %all-to-all-start = ((f32[64,1,1]{2,1,0:T(1,128)}), f32[64,1,1]{2,1,0:T(1,128)S(1)}, u32[]{:S(2)}, u32[]{:S(2)}) async-start(f32[64,1,1]{2,1,0:T(1,128)} %broadcast_in_dim.19), calls=%async_computation | async-start | bytes 65536 | tf_op jit(solution)/shard_map/all_to_all | solution.py:11
  23.2 43.9 %all-gather.3.cloned.1.call-start = ((), (), s32[]{:S(2)}) async-start(), calls=%async_computation.5 | async-start | bytes 2359296 | tf_op jit(solution)/shard_map/all_gather | solution.py:46
  35.8 164.9 %all-gather.5.cloned.1.call-start = ((), (), s32[]{:S(2)}) async-start(), calls=%async_computation.6 | async-start | bytes 8519680 | tf_op jit(solution)/shard_map/all_gather | solution.py:60
  73.9 37.6 %all-to-all-start.2 = ((f32[8,256,256]{2,1,0:T(8,128)}), f32[8,256,256]{2,1,0:T(8,128)S(1)}, u32[]{:S(2)}, u32[]{:S(2)}) async-start(f32[8,256,256]{2,1,0:T(8,128)} %broadcast_in_dim.21), calls=%async_computation.2 | async-start | bytes 4194304 | tf_op jit(solution)/shard_map/all_to_all | solution.py:11
  119.6 9.1 %all-to-all-start.4 = ((f32[8,1,256]{2,1,0:T(1,128)}), f32[8,1,256]{2,1,0:T(1,128)S(1)}, u32[]{:S(2)}, u32[]{:S(2)}) async-start(f32[8,1,256]{2,1,0:T(1,128)} %broadcast_in_dim.23), calls=%async_computation.4 | async-start | bytes 16384 | tf_op jit(solution)/shard_map/all_to_all | solution.py:11
  130.2 66.3 %all-to-all-start.3 = ((f32[8,256,256]{2,1,0:T(8,128)}), f32[8,256,256]{2,1,0:T(8,128)}, u32[]{:S(2)}, u32[]{:S(2)}) async-start(f32[8,256,256]{2,1,0:T(8,128)} %broadcast_in_dim.22), calls=%async_computation.3 | async-start | bytes 4194304 | tf_op jit(solution)/shard_map/all_to_all | solution.py:11
  200.6 9.5 %copy-start = (bf16[2048,448]{0,1:T(8,128)(2,1)S(1)}, bf16[2048,448]{0,1:T(8,128)(2,1)}, u32[]{:S(2)}) copy-start(bf16[2048,448]{0,1:T(8,128)(2,1)} %param.3) | copy-start | bytes 5505028
Sparse Core Ops, SparseCore 0:
  35.9 31.2 all-gather.2
  70.4 125.2 all-gather.4
where the time goes:
time: 233 us; the launch traced here: 232 us
  waiting for transfers between devices  105 us (45%)
  starting transfers between devices  31.2 us (13%)
  blocking collectives  29.3 us (13%)
  matrix products  28.9 us (12%)
  local copies, waits for them, and re-layouts  18.2 us (8%)
  between operations  14.9 us (6%)
  other arithmetic  4.62 us (2%)
    all_to_all x4, waiting for transfers between devices, copy_for_each(): return lax.all_to_all(copies, axis, split_axis=0, concat_axis=0, tiled=True)  103 us
    all_to_all x4, starting transfers between devices, copy_for_each(): return lax.all_to_all(copies, axis, split_axis=0, concat_axis=0, tiled=True)  31.2 us
    all_to_all x1, blocking collectives, copy_for_each(): return lax.all_to_all(copies, axis, split_axis=0, concat_axis=0, tiled=True)  29.3 us
    dot_general x1, matrix products, local(): jnp.einsum('aijc,jcf->iaf', arranged, grad_split, preferred_element_type=...  13.9 us
    unnamed x3, local copies, waits for them, and re-layouts  9.52 us
    dot_general x1, matrix products, local(): jnp.dot(square_rows, m_cols, precision=highest, preferred_element_type=jn...  5.69 us
    dot_general x1, matrix products, local(): jnp.dot(t_rows, t_cols, precision=highest, preferred_element_type=jnp.flo...  5.18 us
    broadcast_in_dim x5, local copies, waits for them, and re-layouts, copy_for_each(): copies = jnp.broadcast_to(x, (lax.axis_size(axis), *x.shape))  5.09 us
  transfers between devices with their start and end apart: 6, of which 5 were waited for; matrix products, arithmetic and copies ran while one was open for 9% of the time, Pallas kernels for 0%

commit v1 on v0

v1 whole, which is shorter than its diff:
```python
import jax
import jax.numpy as jnp
from jax import lax
from jax.experimental import pallas as pl
from jax.experimental.pallas import tpu as pltpu
from jax.sharding import PartitionSpec as P

BLOCK = 2048
SIDE = 256
HALF = 128
ROWS = 144
GRID = 8
F32 = jnp.float32
BF16 = jnp.bfloat16


def eye_mask(n):
    a = lax.broadcasted_iota(jnp.int32, (n, n), 0)
    b = lax.broadcasted_iota(jnp.int32, (n, n), 1)
    return a, b


def three_parts(x):
    hi = x.astype(BF16)
    rest = x - hi.astype(F32)
    mid = rest.astype(BF16)
    low = (rest - mid.astype(F32)).astype(BF16)
    return [hi.astype(F32), mid.astype(F32), low.astype(F32)]


def prep_body(where_ref, s_ref, out_ref):
    row, col = where_ref[0], where_ref[1]
    copies = out_ref.shape[0]
    s = s_ref[...]
    a, b = eye_mask(SIDE)
    squares = jnp.sum(s * s, axis=0, keepdims=True)
    diag = jnp.sum(jnp.where((a == b) & (row == col), s, 0.0), axis=0, keepdims=True)
    tail = three_parts(diag) + three_parts(squares) + [jnp.zeros((ROWS - HALF - 6, SIDE), F32)]
    tail = jnp.concatenate(tail, axis=0).astype(BF16)

    def put(half):
        half = half.astype(BF16)
        for n in range(copies):
            out_ref[n, :HALF, :] = half
            out_ref[n, HALF:, :] = tail

    @pl.when(row < col)
    def _():
        put(s[:HALF, :])

    @pl.when(row > col)
    def _():
        put(s[:, HALF:].T)

    @pl.when(row == col)
    def _():
        p, q = eye_mask(HALF)
        upper = jnp.where(p < q, s[:HALF, :HALF], 0.0)
        lower = jnp.where(p > q, s[HALF:, HALF:], 0.0)
        put(jnp.concatenate([upper + lower, s[:HALF, HALF:]], axis=1))


def prep(where, statistic, copies):
    return pl.pallas_call(
        prep_body,
        out_shape=jax.ShapeDtypeStruct((copies, ROWS, SIDE), BF16),
        in_specs=[
            pl.BlockSpec(memory_space=pltpu.SMEM),
            pl.BlockSpec(memory_space=pltpu.VMEM),
        ],
        out_specs=pl.BlockSpec(memory_space=pltpu.VMEM),
    )(where, statistic)


def block_of(size, index):
    return pl.ds(pl.multiple_of(index * size, size), size)


def main_body(where_ref, own_ref, other_ref, g_ref, m_ref, pre_ref, nd_ref, o_ref, dcol_ref,
              v_ref, t_ref, th_ref, third_ref, oa_ref, ob_ref):
    row, col, core = where_ref[0], where_ref[1], where_ref[2]
    a, b = eye_mask(SIDE)
    same = a == b
    p, q = eye_mask(HALF)
    twin = [own_ref, other_ref]

    def piece(i, j, rows):
        src = twin[j % 2]
        return src[j // 2, i, rows, :]

    squares = jnp.zeros((1, SIDE), F32)
    drows = []
    for i in range(GRID):
        for j in range(GRID):
            tail = piece(i, j, slice(HALF, ROWS)).astype(F32)
            squares = squares + (tail[3:4] + tail[4:5] + tail[5:6])
            if i == j:
                drow = tail[0:1] + tail[1:2] + tail[2:3]
                drows.append(drow)
                dcol_ref[i * SIDE : (i + 1) * SIDE, :] = jnp.sum(
                    jnp.where(same, drow, 0.0), axis=1, keepdims=True
                )
    total = jnp.sum(squares)
    ss = jnp.full((1, 1), total, F32)
    scale = jnp.sqrt(BLOCK * (ss / (BLOCK * BLOCK) + 1e-06))
    inv = 1.0 / scale
    for i in range(GRID):
        here = slice(i * SIDE, (i + 1) * SIDE)
        both = piece(i, i, slice(0, HALF))
        mixed = both[:, :HALF].astype(F32)
        corner = both[:, HALF:]
        upper = jnp.where(p < q, mixed, 0.0)
        lower = jnp.where(p > q, mixed, 0.0)
        o_ref[i * SIDE : i * SIDE + HALF, i * SIDE : i * SIDE + HALF] = (upper + upper.T).astype(BF16)
        o_ref[i * SIDE + HALF : (i + 1) * SIDE, i * SIDE + HALF : (i + 1) * SIDE] = (
            lower + lower.T
        ).astype(BF16)
        o_ref[i * SIDE : i * SIDE + HALF, i * SIDE + HALF : (i + 1) * SIDE] = corner
        o_ref[i * SIDE + HALF : (i + 1) * SIDE, i * SIDE : i * SIDE + HALF] = corner.T
        for j in range(i + 1, GRID):
            there = slice(j * SIDE, (j + 1) * SIDE)
            block = jnp.concatenate(
                [piece(i, j, slice(0, HALF)), piece(j, i, slice(0, HALF))], axis=0
            )
            o_ref[here, there] = block
            o_ref[there, here] = block.T

    v_ref[:, :SIDE] = o_ref[:, block_of(SIDE, row)]
    v_ref[:, SIDE:] = o_ref[:, block_of(SIDE, col)]

    def row_of(index):
        return jnp.sum(jnp.where(same, dcol_ref[block_of(SIDE, index), :], 0.0), axis=0, keepdims=True)

    d_cols = jnp.concatenate([row_of(row), row_of(col)], axis=1)
    lanes = lax.broadcasted_iota(jnp.int32, (SIDE, 2 * SIDE), 1)
    col_ids = jnp.where(lanes < SIDE, row * SIDE + lanes, (col - 1) * SIDE + lanes)
    sub = lax.broadcasted_iota(jnp.int32, (SIDE, 2 * SIDE), 0)

    def two(n, _):
        rows = block_of(SIDE, n)
        w = jnp.dot(o_ref[rows, :], v_ref[...], preferred_element_type=F32)
        o = v_ref[rows, :].astype(F32)
        d = dcol_ref[rows, :]
        on = (sub + n * SIDE) == col_ids
        sq = jnp.where(on, d * d, 0.0) + (d + d_cols) * o + w
        mine = jnp.where(on, d, 0.0) + o
        t = (jnp.where(on, 25.0, 0.0) - (10.0 * inv) * mine + (inv * inv) * sq) * 0.0625
        t_ref[rows, :] = t
        th_ref[rows, :] = jnp.where(on, 0.0, t).astype(BF16)
        return 0

    lax.fori_loop(0, GRID, two, 0)

    own_t = jnp.concatenate([t_ref[block_of(SIDE, row), :SIDE], t_ref[block_of(SIDE, col), SIDE:]], axis=1)
    e_cols = jnp.sum(
        jnp.where(jnp.concatenate([same, same], axis=1), own_t, 0.0), axis=0, keepdims=True
    )

    def three(n, acc):
        rows = block_of(SIDE, n)
        w = jnp.dot(o_ref[rows, :], th_ref[...], preferred_element_type=F32)
        o = v_ref[rows, :].astype(F32)
        t = t_ref[rows, :]
        third = (dcol_ref[rows, :] * t + o * e_cols + w) * inv
        third_ref[rows, :] = third[:, SIDE:]
        on = (sub + n * SIDE) == col_ids
        ob_ref[rows, :] = jnp.where(on, 0.0, third)[:, SIDE:].astype(BF16)
        return acc + jnp.sum(t[:, :SIDE] * third[:, :SIDE], axis=0, keepdims=True)

    nd_ref[...] = lax.fori_loop(0, GRID, three, jnp.zeros((1, SIDE), F32))

    inner = lax.dot_general(
        th_ref[:, :SIDE], ob_ref[...], (((0,), (0,)), ((), ())), preferred_element_type=F32
    )
    e_row = jnp.sum(jnp.where(same, t_ref[block_of(SIDE, row), :SIDE], 0.0), axis=1, keepdims=True)
    third_col = jnp.sum(
        jnp.where(same, third_ref[block_of(SIDE, col), :], 0.0), axis=0, keepdims=True
    )
    full = e_row * third_ref[block_of(SIDE, row), :] + t_ref[block_of(SIDE, row), SIDE:] * third_col + inner
    m_ref[...] = jnp.where(same & (row == col), 0.0, full)

    root = lax.rsqrt(jnp.sqrt(scale))

    def spread(n, _):
        rows = block_of(SIDE, n)
        w = jnp.dot(o_ref[rows, :], g_ref[...], preferred_element_type=F32)
        g = g_ref[rows, :].astype(F32)
        w = w + dcol_ref[rows, :] * g
        pre_ref[rows, :] = ((1.25 * g - (0.25 * inv) * w) * root).astype(BF16)
        return 0

    lax.fori_loop(0, GRID, spread, 0)


def main(where, own, other, gradient):
    wide = gradient.shape[1]
    vmem = pl.BlockSpec(memory_space=pltpu.VMEM)
    return pl.pallas_call(
        main_body,
        out_shape=(
            jax.ShapeDtypeStruct((SIDE, SIDE), F32),
            jax.ShapeDtypeStruct((BLOCK, wide), BF16),
            jax.ShapeDtypeStruct((1, SIDE), F32),
        ),
        in_specs=[pl.BlockSpec(memory_space=pltpu.SMEM), vmem, vmem, vmem],
        out_specs=(vmem, vmem, vmem),
        scratch_shapes=[
            pltpu.VMEM((BLOCK, BLOCK), BF16),
            pltpu.VMEM((BLOCK, 1), F32),
            pltpu.VMEM((BLOCK, 2 * SIDE), BF16),
            pltpu.VMEM((BLOCK, 2 * SIDE), F32),
            pltpu.VMEM((BLOCK, 2 * SIDE), BF16),
            pltpu.VMEM((BLOCK, SIDE), F32),
            pltpu.VMEM((8, 128), BF16),
            pltpu.VMEM((BLOCK, SIDE), BF16),
        ],
        compiler_params=pltpu.CompilerParams(vmem_limit_bytes=56 * 1024 * 1024),
    )(where, own, other, gradient)


SAME_CORE = [[0, 2, 4, 6], [1, 3, 5, 7]]


def local(statistic, gradient):
    row, col = lax.axis_index("row"), lax.axis_index("col")
    core = lax.rem(col, 2)
    where = jnp.stack([row, col, core]).astype(jnp.int32)
    mine = prep(where, statistic, GRID)
    along = lax.all_to_all(mine, "row", split_axis=0, concat_axis=0, tiled=True)
    sent = jnp.broadcast_to(along, (4, *along.shape))
    own = lax.all_to_all(
        sent, "col", split_axis=0, concat_axis=0, tiled=True, axis_index_groups=SAME_CORE
    )
    twin = lax.ppermute(own, "col", [(i, i ^ 1) for i in range(8)])
    even = jnp.where(core == 0, own, twin)
    odd = jnp.where(core == 0, twin, own)
    next_m, preconditioned, next_diag = main(where, even, odd, gradient)
    return (next_m, preconditioned, next_diag.reshape(SIDE))


def solution(mesh):
    return jax.shard_map(
        local,
        mesh=mesh,
        in_specs=(P(("section", "row"), "col"), P("section", ("row", "col"))),
        out_specs=(
            P(("section", "row"), "col"),
            P("section", ("row", "col")),
            P(("section", "row")),
        ),
        check_vma=False,
    )
```

time: 233 us -> 103 us (0.44)
  waiting for transfers between devices: 105 us -> 0.44 us
  matrix products: 28.9 us -> 0 us
  Pallas kernels: 0 us -> 27.9 us
  blocking collectives: 29.3 us -> 57.1 us
  starting transfers between devices: 31.2 us -> 3.48 us
  between operations: 14.9 us -> 0.65 us
  local copies, waits for them, and re-layouts: 18.2 us -> 7.88 us
    all_to_all x4 -> x0, waiting for transfers between devices: 103 us -> none  [copy_for_each(): return lax.all_to_all(copies, axis, split_axis=0, concat_axis=0, tiled=True)]
    all_to_all x4 -> x0, starting transfers between devices: 31.2 us -> none  [copy_for_each(): return lax.all_to_all(copies, axis, split_axis=0, concat_axis=0, tiled=True)]
    dot_general x4 -> x0, matrix products: 28.9 us -> none  [the longest x1 13.9 us: local(): jnp.einsum('aijc,jcf->iaf', arranged, grad_split, preferred_element_type=...]
    pallas_call x0 -> x2, Pallas kernels: none -> 27.9 us  [the longest x1 26 us: main(): pl.pallas_call(main_body, out_shape=(jax.ShapeDtypeStruct((SIDE, SIDE), F...]
    all_to_all x1 -> x2, blocking collectives: 29.3 us -> 57.1 us  [the longest x1 30.5 us: local(): lax.all_to_all(sent, 'col', split_axis=0, concat_axis=0, tiled=True, axis...]
    broadcast_in_dim x5 -> x1, local copies, waits for them, and re-layouts: 5.09 us -> 0.17 us  [local(): sent = jnp.broadcast_to(along, (4, *along.shape))]
    select_n x0 -> x1, other arithmetic: none -> 4.09 us  [local(): odd = jnp.where(core == 0, twin, own)]
    ppermute x0 -> x1, starting transfers between devices: none -> 3.48 us  [local(): twin = lax.ppermute(own, 'col', [(i, i ^ 1) for i in range(8)])]
  transfers between devices with their start and end apart: 6 -> 1, of which waited for: 5 -> 1; matrix products, arithmetic and copies ran while one was open for 9% -> 4% of each run, Pallas kernels for 0% -> 0%
where the time goes in v1:
time: 103 us; the launch traced here: 102 us
  blocking collectives  57.1 us (55%)
  Pallas kernels  27.9 us (27%)
  local copies, waits for them, and re-layouts  7.88 us (8%)
  other arithmetic  4.68 us (5%)
  starting transfers between devices  3.48 us (3%)
    all_to_all x1, blocking collectives, local(): lax.all_to_all(sent, 'col', split_axis=0, concat_axis=0, tiled=True, axis...  30.5 us
    all_to_all x1, blocking collectives, local(): along = lax.all_to_all(mine, 'row', split_axis=0, concat_axis=0, tiled=True)  26.6 us
    pallas_call x1, Pallas kernels, main(): pl.pallas_call(main_body, out_shape=(jax.ShapeDtypeStruct((SIDE, SIDE), F...  26 us
    unnamed x2, local copies, waits for them, and re-layouts  7.7 us
    select_n x1, other arithmetic, local(): odd = jnp.where(core == 0, twin, own)  4.09 us
    ppermute x1, starting transfers between devices, local(): twin = lax.ppermute(own, 'col', [(i, i ^ 1) for i in range(8)])  3.48 us
  transfers between devices with their start and end apart: 1, of which 1 were waited for; matrix products, arithmetic and copies ran while one was open for 4% of the time, Pallas kernels for 0%

profile of v1, /device:TPU:1, one launch (start us, length us, event | category | flops | bytes accessed | tf_op | source)
XLA Modules:
  0.0 102.1 jit_solution(2491106346698075179)
XLA Ops:
  0.6 0.6 pad_add_fusion.where_ref
  1.2 1.9 %shard_map.49 = bf16[8,144,256]{2,1,0:T(8,128)(2,1)} custom-call(s32[3]{0:T(128)} %pad_add_fusion.where_ref, f32[256,256]{1,0:T(8,128)} %s_ref.1), custom_call_target="tpu_custom_call" | custom-call | tf_op jit(solution)/shard_map/pallas_call | solution.py:64
  3.1 26.6 %all_to_all.10 = bf16[8,144,256]{2,1,0:T(8,128)(2,1)S(1)} all-to-all(bf16[8,144,256]{2,1,0:T(8,128)(2,1)} %shard_map.49), channel_id=1, replica_groups=mesh['section'=4,'row'=8,'col'=8] {'row'}, dimensions={0} | all-to-all | bytes 1179648 | tf_op jit(solution)/shard_map/all_to_all | solution.py:229
  29.7 0.2 broadcast_in_dim.3
  29.9 30.5 %all_to_all.11 = bf16[4,8,144,256]{3,2,1,0:T(8,128)(2,1)S(1)} all-to-all(bf16[4,8,144,256]{3,2,1,0:T(8,128)(2,1)S(1)} %broadcast_in_dim.3), channel_id=1, replica_groups={{0,2,4,6},{1,3,5,7},{8,10,12,14},{9,11,13,15},{16,18,20,22},{17,19,21,2..., dimensions={0} | all-to-all | bytes 4718592 | tf_op jit(solution)/shard_map/all_to_all | solution.py:231
  60.4 3.5 %collective-permute-start = (bf16[4,8,144,256]{3,2,1,0:T(8,128)(2,1)S(1)}, bf16[4,8,144,256]{3,2,1,0:T(8,128)(2,1)}, u32[]{:S(2)}, u32[]{:S(2)}) collective-permute-start(bf16[4,8,144,256]{3,2,1,0:T(8,128)(2,1)S(1)} %all_to_all.11), channel_id=1, source_target_pairs={{0,1},{1,0},{2,3},{3,2},{4,5},{5,4},{6,7},{7,6},{8,9},{9,8},{10,11... | collective-permute-start | bytes 7077896 | tf_op jit(solution)/shard_map/ppermute | solution.py:234
  63.9 3.9 %copy.5.g_ref = bf16[2048,448]{1,0:T(8,128)(2,1)} copy(bf16[2048,448]{0,1:T(8,128)(2,1)} %param.3) | data formatting | bytes 3670016 | tf_op args[1]
  67.7 0.4 collective-permute-done
  68.2 4.1 %broadcast_select_fusion = (bf16[4,8,144,256]{3,2,1,0:T(8,128)(2,1)}, bf16[4,8,144,256]{3,2,1,0:T(8,128)(2,1)}) fusion(bf16[4,8,144,256]{3,2,1,0:T(8,128)(2,1)} %collective-permute-done, bf16[4,8,144,256]{3,2,1,0:T(8,128)(2,1)S(1)} %all_to_all.11, pred[]{:T(512)S(6)} %eq.4), kind=kLoop, calls=%fused_computation | loop fusion | flops 2359296 | bytes 9437185 | tf_op jit(solution)/shard_map/jit(_where)/select_n | solution.py:236
  72.3 26.0 %shard_map.50 = (f32[256,256]{1,0:T(8,128)}, bf16[2048,448]{1,0:T(8,128)(2,1)}, f32[1,256]{1,0:T(1,128)}) custom-call(s32[3]{0:T(128)} %pad_add_fusion.where_ref, bf16[4,8,144,256]{3,2,1,0:T(8,128)(2,1)} %get-tuple-element.13.own_ref, bf16[4,8,144,256]{3,2,1,0:T(8,128)(2,1)} %get-tuple-element.12.other_ref, bf16[2048,448]{1,0:T(8,128)(2,1)} %copy.5.g_ref), custom_call_target="tpu_custom_call" | custom-call | tf_op jit(solution)/shard_map/pallas_call | solution.py:198
  98.3 3.8 %copy.6 = bf16[2048,448]{0,1:T(8,128)(2,1)} copy(bf16[2048,448]{1,0:T(8,128)(2,1)} %get-tuple-element.10) | data formatting | bytes 3670016
Async XLA Ops:
  60.4 7.8 %collective-permute-start = (bf16[4,8,144,256]{3,2,1,0:T(8,128)(2,1)S(1)}, bf16[4,8,144,256]{3,2,1,0:T(8,128)(2,1)}, u32[]{:S(2)}, u32[]{:S(2)}) collective-permute-start(bf16[4,8,144,256]{3,2,1,0:T(8,128)(2,1)S(1)} %all_to_all.11), channel_id=1, source_target_pairs={{0,1},{1,0},{2,3},{3,2},{4,5},{5,4},{6,7},{7,6},{8,9},{9,8},{10,11... | collective-permute-start | bytes 7077896 | tf_op jit(solution)/shard_map/ppermute | solution.py:234

commit v2 on v1

v2 whole, which is shorter than its diff:
```python
import jax
import jax.numpy as jnp
from jax import lax
from jax.experimental import pallas as pl
from jax.experimental.pallas import tpu as pltpu
from jax.sharding import PartitionSpec as P

BLOCK = 2048
SIDE = 256
HALF = 128
ROWS = 144
GRID = 8
F32 = jnp.float32
BF16 = jnp.bfloat16


def eye_mask(n):
    a = lax.broadcasted_iota(jnp.int32, (n, n), 0)
    b = lax.broadcasted_iota(jnp.int32, (n, n), 1)
    return a, b


def three_parts(x):
    hi = x.astype(BF16)
    rest = x - hi.astype(F32)
    mid = rest.astype(BF16)
    low = (rest - mid.astype(F32)).astype(BF16)
    return [hi.astype(F32), mid.astype(F32), low.astype(F32)]


def prep_body(where_ref, s_ref, out_ref):
    row, col = where_ref[0], where_ref[1]
    s = s_ref[...]
    a, b = eye_mask(SIDE)
    squares = jnp.sum(s * s, axis=0, keepdims=True)
    diag = jnp.sum(jnp.where((a == b) & (row == col), s, 0.0), axis=0, keepdims=True)
    tail = three_parts(diag) + three_parts(squares) + [jnp.zeros((ROWS - HALF - 6, SIDE), F32)]
    out_ref[HALF:, :] = jnp.concatenate(tail, axis=0).astype(BF16)

    @pl.when(row < col)
    def _():
        out_ref[:HALF, :] = s[:HALF, :].astype(BF16)

    @pl.when(row > col)
    def _():
        out_ref[:HALF, :] = s[:, HALF:].T.astype(BF16)

    @pl.when(row == col)
    def _():
        p, q = eye_mask(HALF)
        upper = jnp.where(p < q, s[:HALF, :HALF], 0.0)
        lower = jnp.where(p > q, s[HALF:, HALF:], 0.0)
        out_ref[:HALF, :HALF] = (upper + lower).astype(BF16)
        out_ref[:HALF, HALF:] = s[:HALF, HALF:].astype(BF16)


def prep(where, statistic):
    return pl.pallas_call(
        prep_body,
        out_shape=jax.ShapeDtypeStruct((ROWS, SIDE), BF16),
        in_specs=[
            pl.BlockSpec(memory_space=pltpu.SMEM),
            pl.BlockSpec(memory_space=pltpu.VMEM),
        ],
        out_specs=pl.BlockSpec(memory_space=pltpu.VMEM),
    )(where, statistic)


def block_of(size, index):
    return pl.ds(pl.multiple_of(index * size, size), size)


TILE = 512


def main_body(where_ref, own_ref, twin_ref, g_hbm, m_ref, pre_hbm, nd_ref, h_ref, g_ref, pre_ref,
              o_ref, dcol_ref, drow_ref, v_ref, t_ref, th_ref, third_ref, ob_ref, in_sem, out_sem):
    row, col, core = where_ref[0], where_ref[1], where_ref[2]
    a, b = eye_mask(SIDE)
    same = a == b
    p, q = eye_mask(HALF)
    arrivals = [
        pltpu.make_async_copy(own_ref, h_ref.at[core], in_sem.at[0]),
        pltpu.make_async_copy(twin_ref, h_ref.at[1 - core], in_sem.at[1]),
        pltpu.make_async_copy(g_hbm, g_ref, in_sem.at[2]),
    ]
    for copy in arrivals:
        copy.start()

    def ring_slot(offset, size):
        middle = size // 2
        return jnp.where(
            offset < middle, 2 * offset, jnp.where(offset == middle, size - 1, 2 * (size - offset) - 1)
        )

    row_slot = [ring_slot(lax.rem(i - row + GRID, GRID), GRID) for i in range(GRID)]
    pair = col // 2
    pair_slot = [ring_slot(lax.rem(j - pair + 4, 4), 4) for j in range(4)]

    def piece(i, j, rows):
        return h_ref[j % 2, pair_slot[j // 2] * GRID + row_slot[i], rows, :]

    arrivals[0].wait()
    arrivals[1].wait()

    squares = jnp.zeros((1, SIDE), F32)
    for i in range(GRID):
        here = slice(i * SIDE, (i + 1) * SIDE)
        for j in range(GRID):
            tail = piece(i, j, slice(HALF, ROWS)).astype(F32)
            squares = squares + (tail[3:4] + tail[4:5] + tail[5:6])
            if i == j:
                drow = tail[0:1] + tail[1:2] + tail[2:3]
                drow_ref[:, here] = drow
                dcol_ref[here, :] = jnp.sum(jnp.where(same, drow, 0.0), axis=1, keepdims=True)
    ss = jnp.full((1, 1), jnp.sum(squares), F32)
    scale = jnp.sqrt(BLOCK * (ss / (BLOCK * BLOCK) + 1e-06))
    inv = 1.0 / scale
    root = lax.rsqrt(jnp.sqrt(scale))
    for i in range(GRID):
        here = slice(i * SIDE, (i + 1) * SIDE)
        first = slice(i * SIDE, i * SIDE + HALF)
        second = slice(i * SIDE + HALF, (i + 1) * SIDE)
        both = piece(i, i, slice(0, HALF))
        mixed = both[:, :HALF].astype(F32)
        corner = both[:, HALF:]
        upper = jnp.where(p < q, mixed, 0.0)
        lower = jnp.where(p > q, mixed, 0.0)
        o_ref[first, first] = (upper + upper.T).astype(BF16)
        o_ref[second, second] = (lower + lower.T).astype(BF16)
        o_ref[first, second] = corner
        o_ref[second, first] = corner.T
        for j in range(i + 1, GRID):
            there = slice(j * SIDE, (j + 1) * SIDE)
            block = jnp.concatenate(
                [piece(i, j, slice(0, HALF)), piece(j, i, slice(0, HALF))], axis=0
            )
            o_ref[here, there] = block
            o_ref[there, here] = block.T

    arrivals[2].wait()

    def leave(n):
        cols = block_of(TILE, n)
        return pltpu.make_async_copy(pre_ref.at[:, cols], pre_hbm.at[:, cols], out_sem.at[n])

    def spread(n, _):
        cols = block_of(TILE, n)
        w = jnp.dot(g_ref[...], o_ref[:, cols], preferred_element_type=F32)
        g = g_ref[:, cols].astype(F32)
        near = (1.25 * root) - (0.25 * inv * root) * drow_ref[:, cols]
        pre_ref[:, cols] = (near * g - (0.25 * inv * root) * w).astype(BF16)
        leave(n).start()
        return 0

    lax.fori_loop(0, BLOCK // TILE, spread, 0)

    v_ref[:, :SIDE] = o_ref[:, block_of(SIDE, row)]
    v_ref[:, SIDE:] = o_ref[:, block_of(SIDE, col)]
    d_cols = jnp.concatenate([drow_ref[:, block_of(SIDE, row)], drow_ref[:, block_of(SIDE, col)]], axis=1)
    lanes = lax.broadcasted_iota(jnp.int32, (TILE, 2 * SIDE), 1)
    col_ids = jnp.where(lanes < SIDE, row * SIDE + lanes, (col - 1) * SIDE + lanes)
    sub = lax.broadcasted_iota(jnp.int32, (TILE, 2 * SIDE), 0)

    def two(n, _):
        rows = block_of(TILE, n)
        w = jnp.dot(o_ref[rows, :], v_ref[...], preferred_element_type=F32)
        o = v_ref[rows, :].astype(F32)
        d = dcol_ref[rows, :]
        on = (sub + n * TILE) == col_ids
        sq = jnp.where(on, d * d, 0.0) + (d + d_cols) * o + w
        mine = jnp.where(on, d, 0.0) + o
        t = (jnp.where(on, 25.0, 0.0) - (10.0 * inv) * mine + (inv * inv) * sq) * 0.0625
        t_ref[rows, :] = t
        th_ref[rows, :] = jnp.where(on, 0.0, t).astype(BF16)
        return 0

    lax.fori_loop(0, BLOCK // TILE, two, 0)

    own_t = jnp.concatenate([t_ref[block_of(SIDE, row), :SIDE], t_ref[block_of(SIDE, col), SIDE:]], axis=1)
    e_cols = jnp.sum(
        jnp.where(jnp.concatenate([same, same], axis=1), own_t, 0.0), axis=0, keepdims=True
    )

    def three(n, acc):
        rows = block_of(TILE, n)
        w = jnp.dot(o_ref[rows, :], th_ref[...], preferred_element_type=F32)
        o = v_ref[rows, :].astype(F32)
        t = t_ref[rows, :]
        third = (dcol_ref[rows, :] * t + o * e_cols + w) * inv
        third_ref[rows, :] = third[:, SIDE:]
        on = (sub + n * TILE) == col_ids
        ob_ref[rows, :] = jnp.where(on, 0.0, third)[:, SIDE:].astype(BF16)
        return acc + jnp.sum(t[:, :SIDE] * third[:, :SIDE], axis=0, keepdims=True)

    nd_ref[...] = lax.fori_loop(0, BLOCK // TILE, three, jnp.zeros((1, SIDE), F32))

    inner = lax.dot_general(
        th_ref[:, :SIDE], ob_ref[...], (((0,), (0,)), ((), ())), preferred_element_type=F32
    )
    e_row = jnp.sum(jnp.where(same, t_ref[block_of(SIDE, row), :SIDE], 0.0), axis=1, keepdims=True)
    third_col = jnp.sum(
        jnp.where(same, third_ref[block_of(SIDE, col), :], 0.0), axis=0, keepdims=True
    )
    full = e_row * third_ref[block_of(SIDE, row), :] + t_ref[block_of(SIDE, row), SIDE:] * third_col + inner
    m_ref[...] = jnp.where(same & (row == col), 0.0, full)
    for n in range(BLOCK // TILE):
        leave(n).wait()


def main(where, own, twin, gradient):
    wide = gradient.shape[0]
    vmem = pl.BlockSpec(memory_space=pltpu.VMEM)
    hbm = pl.BlockSpec(memory_space=pl.ANY)
    return pl.pallas_call(
        main_body,
        out_shape=(
            jax.ShapeDtypeStruct((SIDE, SIDE), F32),
            jax.ShapeDtypeStruct((wide, BLOCK), BF16),
            jax.ShapeDtypeStruct((1, SIDE), F32),
        ),
        in_specs=[pl.BlockSpec(memory_space=pltpu.SMEM), hbm, hbm, hbm],
        out_specs=(vmem, hbm, vmem),
        scratch_shapes=[
            pltpu.VMEM((2, *own.shape), BF16),
            pltpu.VMEM((wide, BLOCK), BF16),
            pltpu.VMEM((wide, BLOCK), BF16),
            pltpu.VMEM((BLOCK, BLOCK), BF16),
            pltpu.VMEM((BLOCK, 1), F32),
            pltpu.VMEM((1, BLOCK), F32),
            pltpu.VMEM((BLOCK, 2 * SIDE), BF16),
            pltpu.VMEM((BLOCK, 2 * SIDE), F32),
            pltpu.VMEM((BLOCK, 2 * SIDE), BF16),
            pltpu.VMEM((BLOCK, SIDE), F32),
            pltpu.VMEM((BLOCK, SIDE), BF16),
            pltpu.SemaphoreType.DMA((3,)),
            pltpu.SemaphoreType.DMA((BLOCK // TILE,)),
        ],
        compiler_params=pltpu.CompilerParams(vmem_limit_bytes=56 * 1024 * 1024),
    )(where, own, twin, gradient)


def shifted(x, axis, step):
    size = lax.axis_size(axis)
    return lax.ppermute(x, axis, [(i, (i + step) % size) for i in range(size)])


def gathered(half):
    up, down = shifted(half, "row", 1), shifted(half, "row", -1)
    up2, down2 = shifted(half, "row", 2), shifted(half, "row", -2)
    up3, down3 = shifted(up, "row", 2), shifted(down, "row", -2)
    up4 = shifted(up2, "row", 2)
    line = jnp.stack([half, up, down, up2, down2, up3, down3, up4])
    over, under = shifted(line, "col", 2), shifted(line, "col", -2)
    far = [shifted(over[:4], "col", 2), shifted(under[4:], "col", -2)]
    return jnp.concatenate([line, over, under, *far])


def local(statistic, gradient):
    row, col = lax.axis_index("row"), lax.axis_index("col")
    where = jnp.stack([row, col, lax.rem(col, 2)]).astype(jnp.int32)
    own = gathered(prep(where, statistic))
    twin = lax.ppermute(own, "col", [(i, i ^ 1) for i in range(GRID)])
    next_m, preconditioned, next_diag = main(where, own, twin, gradient.T)
    return (next_m, preconditioned.T, next_diag.reshape(SIDE))


def solution(mesh):
    return jax.shard_map(
        local,
        mesh=mesh,
        in_specs=(P(("section", "row"), "col"), P("section", ("row", "col"))),
        out_specs=(
            P(("section", "row"), "col"),
            P("section", ("row", "col")),
            P(("section", "row")),
        ),
        check_vma=False,
    )
```

time: 103 us -> 81 us (0.79)
  blocking collectives: 57.1 us -> 0 us
  waiting for transfers between devices: 0.44 us -> 27.3 us
  starting transfers between devices: 3.48 us -> 24.5 us
  local copies, waits for them, and re-layouts: 7.88 us -> 2.65 us
  other arithmetic: 4.68 us -> 0.61 us
  Pallas kernels: 27.9 us -> 24.8 us
    all_to_all x2 -> x0, blocking collectives: 57.1 us -> none  [the longest x1 30.5 us: local(): lax.all_to_all(sent, 'col', split_axis=0, concat_axis=0, tiled=True, axis...]
    ppermute x1 -> x12, waiting for transfers between devices: 0.44 us -> 27.3 us  [the longest x11 23.1 us: shifted(): return lax.ppermute(x, axis, [(i, (i + step) % size) for i in range(size)])]
    ppermute x1 -> x12, starting transfers between devices: 3.48 us -> 24.5 us  [the longest x11 19.4 us: shifted(): return lax.ppermute(x, axis, [(i, (i + step) % size) for i in range(size)])]
    unnamed x2 -> x14, local copies, waits for them, and re-layouts: 7.7 us -> 2.57 us
    select_n x1 -> x0, other arithmetic: 4.09 us -> none  [local(): odd = jnp.where(core == 0, twin, own)]
    pallas_call x1, Pallas kernels: 26 us -> 23.2 us  [main(): pl.pallas_call(main_body, out_shape=(jax.ShapeDtypeStruct((SIDE, SIDE), F...]
  transfers between devices with their start and end apart: 1 -> 12, of which waited for: 1 -> 5; matrix products, arithmetic and copies ran while one was open for 4% -> 1% of each run, Pallas kernels for 0% -> 0%
where the time goes in v2:
time: 81 us; the launch traced here: 80.8 us
  waiting for transfers between devices  27.3 us (34%)
  Pallas kernels  24.8 us (31%)
  starting transfers between devices  24.5 us (30%)
  local copies, waits for them, and re-layouts  2.65 us (3%)
  between operations  0.93 us (1%)
    pallas_call x1, Pallas kernels, main(): pl.pallas_call(main_body, out_shape=(jax.ShapeDtypeStruct((SIDE, SIDE), F...  23.2 us
    ppermute x11, waiting for transfers between devices, shifted(): return lax.ppermute(x, axis, [(i, (i + step) % size) for i in range(size)])  23.1 us
    ppermute x11, starting transfers between devices, shifted(): return lax.ppermute(x, axis, [(i, (i + step) % size) for i in range(size)])  19.4 us
    ppermute x1, starting transfers between devices, local(): twin = lax.ppermute(own, 'col', [(i, i ^ 1) for i in range(GRID)])  5.11 us
    ppermute x1, waiting for transfers between devices, local(): twin = lax.ppermute(own, 'col', [(i, i ^ 1) for i in range(GRID)])  4.16 us
    unnamed x14, local copies, waits for them, and re-layouts  2.57 us
    pallas_call x1, Pallas kernels, prep(): pl.pallas_call(prep_body, out_shape=jax.ShapeDtypeStruct((ROWS, SIDE), BF...  1.66 us
  transfers between devices with their start and end apart: 12, of which 5 were waited for; matrix products, arithmetic and copies ran while one was open for 1% of the time, Pallas kernels for 0%

profile of v2, /device:TPU:1, one launch (start us, length us, event | category | flops | bytes accessed | tf_op | source)
XLA Modules:
  0.0 80.8 jit_solution(11388009149208229931)
XLA Ops:
  0.6 0.6 pad_add_fusion.where_ref
  1.2 1.7 %shard_map.49 = bf16[144,256]{1,0:T(8,128)(2,1)} custom-call(s32[3]{0:T(128)} %pad_add_fusion.where_ref, f32[256,256]{1,0:T(8,128)} %s_ref.1), custom_call_target="tpu_custom_call" | custom-call | tf_op jit(solution)/shard_map/pallas_call | solution.py:58
  2.9 6.9 %collective-permute-start.3 = (bf16[144,256]{1,0:T(8,128)(2,1)}, bf16[144,256]{1,0:T(8,128)(2,1)S(1)}, u32[]{:S(2)}, u32[]{:S(2)}) collective-permute-start(bf16[144,256]{1,0:T(8,128)(2,1)} %shard_map.49), channel_id=1, source_target_pairs={{0,48},{8,56},{16,0},{24,8},{32,16},{40,24},{48,32},{56,40},{1,49}... | collective-permute-start | bytes 221192 | tf_op jit(solution)/shard_map/ppermute | solution.py:245
  9.8 0.0 collective-permute-start.2
  9.8 3.1 %collective-permute-start.1 = (bf16[144,256]{1,0:T(8,128)(2,1)}, bf16[144,256]{1,0:T(8,128)(2,1)S(1)}, u32[]{:S(2)}, u32[]{:S(2)}) collective-permute-start(bf16[144,256]{1,0:T(8,128)(2,1)} %shard_map.49), channel_id=1, source_target_pairs={{0,56},{8,0},{16,8},{24,16},{32,24},{40,32},{48,40},{56,48},{1,57}... | collective-permute-start | bytes 221192 | tf_op jit(solution)/shard_map/ppermute | solution.py:245
  13.0 0.0 collective-permute-start
  13.0 1.0 %bitcast_dynamic-update-slice_fusion.15 = (bf16[8,144,256]{2,1,0:T(8,128)(2,1)S(1)}, bf16[32,144,256]{2,1,0:T(8,128)(2,1)S(1)}) fusion(bf16[144,256]{1,0:T(8,128)(2,1)} %shard_map.49), kind=kLoop, calls=%fused_computation.15 | loop fusion | bytes 221184
  13.9 2.4 %collective-permute-done.2 = bf16[144,256]{1,0:T(8,128)(2,1)S(1)} collective-permute-done((bf16[144,256]{1,0:T(8,128)(2,1)}, bf16[144,256]{1,0:T(8,128)(2,1)S(1)}, u32[]{:S(2)}, u32[]{:S(2)}) %collective-permute-start.2) | collective-permute-done | bytes 73760 | tf_op jit(solution)/shard_map/ppermute | solution.py:245
  16.3 0.0 collective-permute-start.6
  16.3 0.0 collective-permute-done.1
  16.3 3.6 %collective-permute-start.5 = (bf16[144,256]{1,0:T(8,128)(2,1)S(1)}, bf16[144,256]{1,0:T(8,128)(2,1)S(1)}, u32[]{:S(2)}, u32[]{:S(2)}) collective-permute-start(bf16[144,256]{1,0:T(8,128)(2,1)S(1)} %collective-permute-done.1), channel_id=1, source_target_pairs={{0,48},{8,56},{16,0},{24,8},{32,16},{40,24},{48,32},{56,40},{1,49}... | collective-permute-start | bytes 221192 | tf_op jit(solution)/shard_map/ppermute | solution.py:245
  19.9 0.0 collective-permute-done
  19.9 0.0 collective-permute-start.4
  20.0 0.0 collective-permute-done.3
  20.0 6.3 %collective-permute-done.4 = bf16[144,256]{1,0:T(8,128)(2,1)S(1)} collective-permute-done((bf16[144,256]{1,0:T(8,128)(2,1)S(1)}, bf16[144,256]{1,0:T(8,128)(2,1)S(1)}, u32[]{:S(2)}, u32[]{:S(2)}) %collective-permute-start.4) | collective-permute-done | bytes 73760 | tf_op jit(solution)/shard_map/ppermute | solution.py:245
  26.3 0.0 collective-permute-done.5
  26.4 0.0 collective-permute-done.6
  26.4 1.8 %collective-permute-start.7 = (bf16[8,144,256]{2,1,0:T(8,128)(2,1)S(1)}, bf16[8,144,256]{2,1,0:T(8,128)(2,1)S(1)}, u32[]{:S(2)}, u32[]{:S(2)}) collective-permute-start(bf16[8,144,256]{2,1,0:T(8,128)(2,1)S(1)} %get-tuple-element.9), channel_id=1, source_target_pairs={{0,2},{1,3},{2,4},{3,5},{4,6},{5,7},{6,0},{7,1},{8,10},{9,11},{10,... | collective-permute-start | bytes 1769480 | tf_op jit(solution)/shard_map/ppermute | solution.py:245
  28.2 1.1 %collective-permute-start.8 = (bf16[8,144,256]{2,1,0:T(8,128)(2,1)S(1)}, bf16[8,144,256]{2,1,0:T(8,128)(2,1)S(1)}, u32[]{:S(2)}, u32[]{:S(2)}) collective-permute-start(bf16[8,144,256]{2,1,0:T(8,128)(2,1)S(1)} %get-tuple-element.9), channel_id=1, source_target_pairs={{0,6},{1,7},{2,0},{3,1},{4,2},{5,3},{6,4},{7,5},{8,14},{9,15},{10,... | collective-permute-start | bytes 1769480 | tf_op jit(solution)/shard_map/ppermute | solution.py:245
  29.3 10.5 %collective-permute-done.7 = bf16[8,144,256]{2,1,0:T(8,128)(2,1)S(1)} collective-permute-done((bf16[8,144,256]{2,1,0:T(8,128)(2,1)S(1)}, bf16[8,144,256]{2,1,0:T(8,128)(2,1)S(1)}, u32[]{:S(2)}, u32[]{:S(2)}) %collective-permute-start.7) | collective-permute-done | bytes 589856 | tf_op jit(solution)/shard_map/ppermute | solution.py:245
  39.9 0.9 %collective-permute-start.9 = (bf16[4,144,256]{2,1,0:T(8,128)(2,1)S(1)}, bf16[4,144,256]{2,1,0:T(8,128)(2,1)S(1)}, u32[]{:S(2)}, u32[]{:S(2)}) collective-permute-start(bf16[4,144,256]{2,1,0:T(8,128)(2,1)S(1)} %slice.8), channel_id=1, source_target_pairs={{0,2},{1,3},{2,4},{3,5},{4,6},{5,7},{6,0},{7,1},{8,10},{9,11},{10,... | collective-permute-start | bytes 884744 | tf_op jit(solution)/shard_map/ppermute | solution.py:245
  40.7 0.0 collective-permute-done.8
  40.8 1.9 %collective-permute-start.10 = (bf16[4,144,256]{2,1,0:T(8,128)(2,1)S(1)}, bf16[4,144,256]{2,1,0:T(8,128)(2,1)S(1)}, u32[]{:S(2)}, u32[]{:S(2)}) collective-permute-start(bf16[4,144,256]{2,1,0:T(8,128)(2,1)S(1)} %slice.9), channel_id=1, source_target_pairs={{0,6},{1,7},{2,0},{3,1},{4,2},{5,3},{6,4},{7,5},{8,14},{9,15},{10,... | collective-permute-start | bytes 884744 | tf_op jit(solution)/shard_map/ppermute | solution.py:245
  42.8 3.9 %collective-permute-done.9 = bf16[4,144,256]{2,1,0:T(8,128)(2,1)S(1)} collective-permute-done((bf16[4,144,256]{2,1,0:T(8,128)(2,1)S(1)}, bf16[4,144,256]{2,1,0:T(8,128)(2,1)S(1)}, u32[]{:S(2)}, u32[]{:S(2)}) %collective-permute-start.9) | collective-permute-done | bytes 294944 | tf_op jit(solution)/shard_map/ppermute | solution.py:245
  46.8 0.0 collective-permute-done.10
  46.8 0.0 copy-start
  46.8 5.1 %collective-permute-start.11 = (bf16[32,144,256]{2,1,0:T(8,128)(2,1)S(1)}, bf16[32,144,256]{2,1,0:T(8,128)(2,1)S(1)}, u32[]{:S(2)}, u32[]{:S(2)}) collective-permute-start(bf16[32,144,256]{2,1,0:T(8,128)(2,1)S(1)} %constant_dynamic-update-slice_fusion.own_ref), channel_id=1, source_target_pairs={{0,1},{1,0},{2,3},{3,2},{4,5},{5,4},{6,7},{7,6},{8,9},{9,8},{10,11... | collective-permute-start | bytes 7077896 | tf_op jit(solution)/shard_map/ppermute | solution.py:263
  51.9 4.2 %collective-permute-done.11.twin_ref = bf16[32,144,256]{2,1,0:T(8,128)(2,1)S(1)} collective-permute-done((bf16[32,144,256]{2,1,0:T(8,128)(2,1)S(1)}, bf16[32,144,256]{2,1,0:T(8,128)(2,1)S(1)}, u32[]{:S(2)}, u32[]{:S(2)}) %collective-permute-start.11) | collective-permute-done | bytes 2359328 | tf_op jit(solution)/shard_map/ppermute | solution.py:263
  56.1 0.0 copy-start.1
  56.1 0.0 copy-done
  56.1 1.4 %copy-done.1 = bf16[32,144,256]{2,1,0:T(8,128)(2,1)} copy-done((bf16[32,144,256]{2,1,0:T(8,128)(2,1)}, bf16[32,144,256]{2,1,0:T(8,128)(2,1)S(1)}, u32[]{:S(2)}) %copy-start.1) | copy-done | bytes 2359320
  57.5 23.2 %shard_map.50 = (f32[256,256]{1,0:T(8,128)}, bf16[448,2048]{1,0:T(8,128)(2,1)}, f32[1,256]{1,0:T(1,128)}) custom-call(s32[3]{0:T(128)} %pad_add_fusion.where_ref, bf16[32,144,256]{2,1,0:T(8,128)(2,1)} %copy-done, bf16[32,144,256]{2,1,0:T(8,128)(2,1)} %copy-done.1, bf16[448,2048]{1,0:T(8,128)(2,1)} %bitcast.30), custom_call_target="tpu_custom_call" | custom-call | tf_op jit(solution)/shard_map/pallas_call | solution.py:215
  (13 shorter events, 0.2 us)
Async XLA Ops:
  2.9 17.1 %collective-permute-start.3 = (bf16[144,256]{1,0:T(8,128)(2,1)}, bf16[144,256]{1,0:T(8,128)(2,1)S(1)}, u32[]{:S(2)}, u32[]{:S(2)}) collective-permute-start(bf16[144,256]{1,0:T(8,128)(2,1)} %shard_map.49), channel_id=1, source_target_pairs={{0,48},{8,56},{16,0},{24,8},{32,16},{40,24},{48,32},{56,40},{1,49}... | collective-permute-start | bytes 221192 | tf_op jit(solution)/shard_map/ppermute | solution.py:245
  9.8 6.5 %collective-permute-start.2 = (bf16[144,256]{1,0:T(8,128)(2,1)}, bf16[144,256]{1,0:T(8,128)(2,1)S(1)}, u32[]{:S(2)}, u32[]{:S(2)}) collective-permute-start(bf16[144,256]{1,0:T(8,128)(2,1)} %shard_map.49), channel_id=1, source_target_pairs={{0,16},{8,24},{16,32},{24,40},{32,48},{40,56},{48,0},{56,8},{1,17}... | collective-permute-start | bytes 221192 | tf_op jit(solution)/shard_map/ppermute | solution.py:245
  9.8 6.5 %collective-permute-start.1 = (bf16[144,256]{1,0:T(8,128)(2,1)}, bf16[144,256]{1,0:T(8,128)(2,1)S(1)}, u32[]{:S(2)}, u32[]{:S(2)}) collective-permute-start(bf16[144,256]{1,0:T(8,128)(2,1)} %shard_map.49), channel_id=1, source_target_pairs={{0,56},{8,0},{16,8},{24,16},{32,24},{40,32},{48,40},{56,48},{1,57}... | collective-permute-start | bytes 221192 | tf_op jit(solution)/shard_map/ppermute | solution.py:245
  13.0 6.9 %collective-permute-start = (bf16[144,256]{1,0:T(8,128)(2,1)}, bf16[144,256]{1,0:T(8,128)(2,1)S(1)}, u32[]{:S(2)}, u32[]{:S(2)}) collective-permute-start(bf16[144,256]{1,0:T(8,128)(2,1)} %shard_map.49), channel_id=1, source_target_pairs={{0,8},{8,16},{16,24},{24,32},{32,40},{40,48},{48,56},{56,0},{1,9},... | collective-permute-start | bytes 221192 | tf_op jit(solution)/shard_map/ppermute | solution.py:245
  16.3 10.1 %collective-permute-start.6 = (bf16[144,256]{1,0:T(8,128)(2,1)S(1)}, bf16[144,256]{1,0:T(8,128)(2,1)S(1)}, u32[]{:S(2)}, u32[]{:S(2)}) collective-permute-start(bf16[144,256]{1,0:T(8,128)(2,1)S(1)} %collective-permute-done.2), channel_id=1, source_target_pairs={{0,16},{8,24},{16,32},{24,40},{32,48},{40,56},{48,0},{56,8},{1,17}... | collective-permute-start | bytes 221192 | tf_op jit(solution)/shard_map/ppermute | solution.py:245
  16.3 10.0 %collective-permute-start.5 = (bf16[144,256]{1,0:T(8,128)(2,1)S(1)}, bf16[144,256]{1,0:T(8,128)(2,1)S(1)}, u32[]{:S(2)}, u32[]{:S(2)}) collective-permute-start(bf16[144,256]{1,0:T(8,128)(2,1)S(1)} %collective-permute-done.1), channel_id=1, source_target_pairs={{0,48},{8,56},{16,0},{24,8},{32,16},{40,24},{48,32},{56,40},{1,49}... | collective-permute-start | bytes 221192 | tf_op jit(solution)/shard_map/ppermute | solution.py:245
  19.9 6.4 %collective-permute-start.4 = (bf16[144,256]{1,0:T(8,128)(2,1)S(1)}, bf16[144,256]{1,0:T(8,128)(2,1)S(1)}, u32[]{:S(2)}, u32[]{:S(2)}) collective-permute-start(bf16[144,256]{1,0:T(8,128)(2,1)S(1)} %collective-permute-done), channel_id=1, source_target_pairs={{0,16},{8,24},{16,32},{24,40},{32,48},{40,56},{48,0},{56,8},{1,17}... | collective-permute-start | bytes 221192 | tf_op jit(solution)/shard_map/ppermute | solution.py:245
  26.4 13.4 %collective-permute-start.7 = (bf16[8,144,256]{2,1,0:T(8,128)(2,1)S(1)}, bf16[8,144,256]{2,1,0:T(8,128)(2,1)S(1)}, u32[]{:S(2)}, u32[]{:S(2)}) collective-permute-start(bf16[8,144,256]{2,1,0:T(8,128)(2,1)S(1)} %get-tuple-element.9), channel_id=1, source_target_pairs={{0,2},{1,3},{2,4},{3,5},{4,6},{5,7},{6,0},{7,1},{8,10},{9,11},{10,... | collective-permute-start | bytes 1769480 | tf_op jit(solution)/shard_map/ppermute | solution.py:245
  28.2 12.5 %collective-permute-start.8 = (bf16[8,144,256]{2,1,0:T(8,128)(2,1)S(1)}, bf16[8,144,256]{2,1,0:T(8,128)(2,1)S(1)}, u32[]{:S(2)}, u32[]{:S(2)}) collective-permute-start(bf16[8,144,256]{2,1,0:T(8,128)(2,1)S(1)} %get-tuple-element.9), channel_id=1, source_target_pairs={{0,6},{1,7},{2,0},{3,1},{4,2},{5,3},{6,4},{7,5},{8,14},{9,15},{10,... | collective-permute-start | bytes 1769480 | tf_op jit(solution)/shard_map/ppermute | solution.py:245
  39.9 6.9 %collective-permute-start.9 = (bf16[4,144,256]{2,1,0:T(8,128)(2,1)S(1)}, bf16[4,144,256]{2,1,0:T(8,128)(2,1)S(1)}, u32[]{:S(2)}, u32[]{:S(2)}) collective-permute-start(bf16[4,144,256]{2,1,0:T(8,128)(2,1)S(1)} %slice.8), channel_id=1, source_target_pairs={{0,2},{1,3},{2,4},{3,5},{4,6},{5,7},{6,0},{7,1},{8,10},{9,11},{10,... | collective-permute-start | bytes 884744 | tf_op jit(solution)/shard_map/ppermute | solution.py:245
  40.8 6.0 %collective-permute-start.10 = (bf16[4,144,256]{2,1,0:T(8,128)(2,1)S(1)}, bf16[4,144,256]{2,1,0:T(8,128)(2,1)S(1)}, u32[]{:S(2)}, u32[]{:S(2)}) collective-permute-start(bf16[4,144,256]{2,1,0:T(8,128)(2,1)S(1)} %slice.9), channel_id=1, source_target_pairs={{0,6},{1,7},{2,0},{3,1},{4,2},{5,3},{6,4},{7,5},{8,14},{9,15},{10,... | collective-permute-start | bytes 884744 | tf_op jit(solution)/shard_map/ppermute | solution.py:245
  46.8 9.3 %copy-start = (bf16[32,144,256]{2,1,0:T(8,128)(2,1)}, bf16[32,144,256]{2,1,0:T(8,128)(2,1)S(1)}, u32[]{:S(2)}) copy-start(bf16[32,144,256]{2,1,0:T(8,128)(2,1)S(1)} %constant_dynamic-update-slice_fusion.own_ref) | copy-start | bytes 7077892
  46.8 9.3 %collective-permute-start.11 = (bf16[32,144,256]{2,1,0:T(8,128)(2,1)S(1)}, bf16[32,144,256]{2,1,0:T(8,128)(2,1)S(1)}, u32[]{:S(2)}, u32[]{:S(2)}) collective-permute-start(bf16[32,144,256]{2,1,0:T(8,128)(2,1)S(1)} %constant_dynamic-update-slice_fusion.own_ref), channel_id=1, source_target_pairs={{0,1},{1,0},{2,3},{3,2},{4,5},{5,4},{6,7},{7,6},{8,9},{9,8},{10,11... | collective-permute-start | bytes 7077896 | tf_op jit(solution)/shard_map/ppermute | solution.py:263
  56.1 1.4 %copy-start.1 = (bf16[32,144,256]{2,1,0:T(8,128)(2,1)}, bf16[32,144,256]{2,1,0:T(8,128)(2,1)S(1)}, u32[]{:S(2)}) copy-start(bf16[32,144,256]{2,1,0:T(8,128)(2,1)S(1)} %collective-permute-done.11.twin_ref) | copy-start | bytes 7077892

commit v3 on v2

v3 whole, which is shorter than its diff:
```python
import jax
import jax.numpy as jnp
from jax import lax
from jax.experimental import pallas as pl
from jax.experimental.pallas import tpu as pltpu
from jax.sharding import PartitionSpec as P

BLOCK = 2048
SIDE = 256
HALF = 128
ROWS = 144
GRID = 8
F32 = jnp.float32
BF16 = jnp.bfloat16


def eye_mask(n):
    a = lax.broadcasted_iota(jnp.int32, (n, n), 0)
    b = lax.broadcasted_iota(jnp.int32, (n, n), 1)
    return a, b


def three_parts(x):
    hi = x.astype(BF16)
    rest = x - hi.astype(F32)
    mid = rest.astype(BF16)
    low = (rest - mid.astype(F32)).astype(BF16)
    return [hi.astype(F32), mid.astype(F32), low.astype(F32)]


def prep_body(s_ref, out_ref):
    row, col = lax.axis_index("row"), lax.axis_index("col")
    s = s_ref[...]
    a, b = eye_mask(SIDE)
    squares = jnp.sum(s * s, axis=0, keepdims=True)
    diag = jnp.sum(jnp.where((a == b) & (row == col), s, 0.0), axis=0, keepdims=True)
    tail = three_parts(diag) + three_parts(squares) + [jnp.zeros((ROWS - HALF - 6, SIDE), F32)]
    out_ref[HALF:, :] = jnp.concatenate(tail, axis=0).astype(BF16)

    @pl.when(row < col)
    def _():
        out_ref[:HALF, :] = s[:HALF, :].astype(BF16)

    @pl.when(row > col)
    def _():
        out_ref[:HALF, :] = s[:, HALF:].T.astype(BF16)

    @pl.when(row == col)
    def _():
        p, q = eye_mask(HALF)
        upper = jnp.where(p < q, s[:HALF, :HALF], 0.0)
        lower = jnp.where(p > q, s[HALF:, HALF:], 0.0)
        out_ref[:HALF, :HALF] = (upper + lower).astype(BF16)
        out_ref[:HALF, HALF:] = s[:HALF, HALF:].astype(BF16)


def prep(statistic):
    return pl.pallas_call(
        prep_body,
        out_shape=jax.ShapeDtypeStruct((ROWS, SIDE), BF16),
        in_specs=[pl.BlockSpec(memory_space=pltpu.VMEM)],
        out_specs=pl.BlockSpec(memory_space=pltpu.VMEM),
    )(statistic)


def block_of(size, index):
    return pl.ds(pl.multiple_of(index * size, size), size)


TILE = 512


def main_body(own_ref, twin_ref, g_hbm, m_ref, pre_hbm, nd_ref, g_ref, pre_ref,
              o_ref, dcol_ref, drow_ref, v_ref, t_ref, th_ref, third_ref, ob_ref,
              in_sem, out_sem):
    row, col = lax.axis_index("row"), lax.axis_index("col")
    core = lax.rem(col, 2)
    a, b = eye_mask(SIDE)
    same = a == b
    p, q = eye_mask(HALF)
    arrival = pltpu.make_async_copy(g_hbm, g_ref, in_sem.at[0])
    arrival.start()

    def ring_slot(offset, size):
        middle = size // 2
        return jnp.where(
            offset < middle, 2 * offset, jnp.where(offset == middle, size - 1, 2 * (size - offset) - 1)
        )

    row_slot = [ring_slot(lax.rem(i - row + GRID, GRID), GRID) for i in range(GRID)]
    pair = col // 2
    pair_slot = [ring_slot(lax.rem(j - pair + 4, 4), 4) for j in range(4)]

    def slot_of(j, line):
        over, under, far = pair_slot[j] == 1, pair_slot[j] == 2, pair_slot[j] == 3
        first = jnp.where(over, 8, jnp.where(under, 13, jnp.where(far, 24, 0)))
        then = jnp.where(over, 13, jnp.where(under, 16, jnp.where(far, 24, 0)))
        return line + jnp.where(line < 5, first, then)

    def above(half, i, there):
        o_ref[i * SIDE : i * SIDE + HALF, there] = half
        o_ref[there, i * SIDE : i * SIDE + HALF] = half.T

    def below(half, second, i):
        o_ref[second, i * SIDE : (i + 1) * SIDE] = half
        o_ref[i * SIDE : (i + 1) * SIDE, second] = half.T

    def middle(half, i):
        first = slice(i * SIDE, i * SIDE + HALF)
        second = slice(i * SIDE + HALF, (i + 1) * SIDE)
        mixed = half[:, :HALF].astype(F32)
        corner = half[:, HALF:]
        upper = jnp.where(p < q, mixed, 0.0)
        lower = jnp.where(p > q, mixed, 0.0)
        o_ref[first, first] = (upper + upper.T).astype(BF16)
        o_ref[second, second] = (lower + lower.T).astype(BF16)
        o_ref[first, second] = corner
        o_ref[second, first] = corner.T

    def assemble(pieces_ref, parity):
        total = jnp.zeros((1, SIDE), F32)
        for j in range(4):
            there = block_of(SIDE, 2 * j + parity)
            second = pl.ds(pl.multiple_of((2 * j + parity) * SIDE + HALF, HALF), HALF)
            for i in range(GRID):
                slot = slot_of(j, row_slot[i])
                tail = pieces_ref[slot, HALF:ROWS, :].astype(F32)
                total = total + (tail[3:4] + tail[4:5] + tail[5:6])
                if i == 2 * j:

                    @pl.when(parity == 0)
                    def _():
                        middle(pieces_ref[slot, :HALF, :], i)

                    @pl.when(parity == 1)
                    def _():
                        above(pieces_ref[slot, :HALF, :], i, there)

                elif i == 2 * j + 1:

                    @pl.when(parity == 1)
                    def _():
                        middle(pieces_ref[slot, :HALF, :], i)

                    @pl.when(parity == 0)
                    def _():
                        below(pieces_ref[slot, :HALF, :], second, i)

                elif i < 2 * j:
                    above(pieces_ref[slot, :HALF, :], i, there)
                else:
                    below(pieces_ref[slot, :HALF, :], second, i)
            slot = slot_of(j, jnp.where(parity == 0, row_slot[2 * j], row_slot[2 * j + 1]))
            tail = pieces_ref[slot, HALF:ROWS, :].astype(F32)
            drow = tail[0:1] + tail[1:2] + tail[2:3]
            drow_ref[:, there] = drow
            dcol_ref[there, :] = jnp.sum(jnp.where(same, drow, 0.0), axis=1, keepdims=True)
        return total

    squares = assemble(own_ref, core) + assemble(twin_ref, 1 - core)
    ss = jnp.full((1, 1), jnp.sum(squares), F32)
    scale = jnp.sqrt(BLOCK * (ss / (BLOCK * BLOCK) + 1e-06))
    inv = 1.0 / scale
    root = lax.rsqrt(jnp.sqrt(scale))

    arrival.wait()

    def leave(n):
        cols = block_of(TILE, n)
        return pltpu.make_async_copy(pre_ref.at[:, cols], pre_hbm.at[:, cols], out_sem.at[n])

    far_by = 0.25 * inv * root

    def spread(n, _):
        cols = block_of(TILE, n)
        w = jnp.dot(g_ref[...], o_ref[:, cols], preferred_element_type=F32)
        near_by = (1.25 * root) - far_by * drow_ref[:, cols]
        pre_ref[:, cols] = (near_by * g_ref[:, cols].astype(F32) - far_by * w).astype(BF16)
        leave(n).start()
        return 0

    lax.fori_loop(0, BLOCK // TILE, spread, 0)

    v_ref[:, :SIDE] = o_ref[:, block_of(SIDE, row)]
    v_ref[:, SIDE:] = o_ref[:, block_of(SIDE, col)]
    d_cols = jnp.concatenate([drow_ref[:, block_of(SIDE, row)], drow_ref[:, block_of(SIDE, col)]], axis=1)
    second_by = 0.0625 * inv * inv
    by_col = second_by * d_cols - 0.625 * inv

    def two(n, _):
        rows = block_of(TILE, n)
        w = jnp.dot(o_ref[rows, :], v_ref[...], preferred_element_type=F32)
        t = (second_by * dcol_ref[rows, :] + by_col) * v_ref[rows, :].astype(F32) + second_by * w
        t_ref[rows, :] = t
        th_ref[rows, :] = t.astype(BF16)
        return 0

    lax.fori_loop(0, BLOCK // TILE, two, 0)

    ones = d_cols * inv
    alone = (25.0 - 10.0 * ones + ones * ones) * 0.0625
    diags = []
    for place, lanes in ((row, slice(0, SIDE)), (col, slice(SIDE, 2 * SIDE))):
        rows = block_of(SIDE, place)
        t = t_ref[rows, lanes] + jnp.where(same, alone[:, lanes], 0.0)
        t_ref[rows, lanes] = t
        th_ref[rows, lanes] = jnp.where(same, 0.0, t).astype(BF16)
        diags.append(jnp.where(same, t, 0.0))
    e_cols = jnp.concatenate([jnp.sum(x, axis=0, keepdims=True) for x in diags], axis=1)
    e_row = jnp.sum(diags[0], axis=1, keepdims=True)
    e_by = e_cols * inv

    def three(n, acc):
        rows = block_of(TILE, n)
        w = jnp.dot(o_ref[rows, :], th_ref[...], preferred_element_type=F32)
        t = t_ref[rows, :]
        third = (dcol_ref[rows, :] * inv) * t + v_ref[rows, :].astype(F32) * e_by + w * inv
        third_ref[rows, :] = third[:, SIDE:]
        ob_ref[rows, :] = third[:, SIDE:].astype(BF16)
        return acc + jnp.sum(t[:, :SIDE] * third[:, :SIDE], axis=0, keepdims=True)

    nd_ref[...] = lax.fori_loop(0, BLOCK // TILE, three, jnp.zeros((1, SIDE), F32))

    rows = block_of(SIDE, col)
    third = third_ref[rows, :]
    ob_ref[rows, :] = jnp.where(same, 0.0, third).astype(BF16)
    third_col = jnp.sum(jnp.where(same, third, 0.0), axis=0, keepdims=True)
    inner = lax.dot_general(
        th_ref[:, :SIDE], ob_ref[...], (((0,), (0,)), ((), ())), preferred_element_type=F32
    )
    rows = block_of(SIDE, row)
    full = e_row * third_ref[rows, :] + t_ref[rows, SIDE:] * third_col + inner
    m_ref[...] = jnp.where(same & (row == col), 0.0, full)
    for n in range(BLOCK // TILE):
        leave(n).wait()


def main(own, twin, gradient):
    wide = gradient.shape[0]
    vmem = pl.BlockSpec(memory_space=pltpu.VMEM)
    hbm = pl.BlockSpec(memory_space=pl.ANY)
    return pl.pallas_call(
        main_body,
        out_shape=(
            jax.ShapeDtypeStruct((SIDE, SIDE), F32),
            jax.ShapeDtypeStruct((wide, BLOCK), BF16),
            jax.ShapeDtypeStruct((1, SIDE), F32),
        ),
        in_specs=[vmem, vmem, hbm],
        out_specs=(vmem, hbm, vmem),
        scratch_shapes=[
            pltpu.VMEM((wide, BLOCK), BF16),
            pltpu.VMEM((wide, BLOCK), BF16),
            pltpu.VMEM((BLOCK, BLOCK), BF16),
            pltpu.VMEM((BLOCK, 1), F32),
            pltpu.VMEM((1, BLOCK), F32),
            pltpu.VMEM((BLOCK, 2 * SIDE), BF16),
            pltpu.VMEM((BLOCK, 2 * SIDE), F32),
            pltpu.VMEM((BLOCK, 2 * SIDE), BF16),
            pltpu.VMEM((BLOCK, SIDE), F32),
            pltpu.VMEM((BLOCK, SIDE), BF16),
            pltpu.SemaphoreType.DMA((1,)),
            pltpu.SemaphoreType.DMA((BLOCK // TILE,)),
        ],
        compiler_params=pltpu.CompilerParams(vmem_limit_bytes=56 * 1024 * 1024),
    )(
        pltpu.with_memory_space_constraint(own, pltpu.VMEM),
        pltpu.with_memory_space_constraint(twin, pltpu.VMEM),
        gradient,
    )


def shifted(x, axis, step):
    size = lax.axis_size(axis)
    return lax.ppermute(x, axis, [(i, (i + step) % size) for i in range(size)])


def gathered(half):
    up, down = shifted(half, "row", 1), shifted(half, "row", -1)
    up2, down2 = shifted(half, "row", 2), shifted(half, "row", -2)
    near = jnp.stack([half, up, down, up2, down2])
    near_over, near_under = shifted(near, "col", 2), shifted(near, "col", -2)
    up3, down3 = shifted(up, "row", 2), shifted(down, "row", -2)
    up4 = shifted(up2, "row", 2)
    rest = jnp.stack([up3, down3, up4])
    rest_over, rest_under = shifted(rest, "col", 2), shifted(rest, "col", -2)
    far = [shifted(near_over, "col", 2), shifted(rest_under, "col", -2)]
    early = jnp.concatenate([near, rest, near_over, near_under])
    late = jnp.concatenate([rest_over, rest_under, *far])
    return early, late


def local(statistic, gradient):
    early, late = gathered(prep(statistic))
    twins = []
    for part in (early, late):
        twins.append(lax.ppermute(part, "col", [(i, i ^ 1) for i in range(GRID)]))
    own, twin = jnp.concatenate([early, late]), jnp.concatenate(twins)
    next_m, preconditioned, next_diag = main(own, twin, gradient.T)
    return (next_m, preconditioned.T, next_diag.reshape(SIDE))


def solution(mesh):
    return jax.shard_map(
        local,
        mesh=mesh,
        in_specs=(P(("section", "row"), "col"), P("section", ("row", "col"))),
        out_specs=(
            P(("section", "row"), "col"),
            P("section", ("row", "col")),
            P(("section", "row")),
        ),
        check_vma=False,
    )
```

time: 81 us -> 70 us (0.86)
  waiting for transfers between devices: 27.3 us -> 13.8 us
  starting transfers between devices: 24.5 us -> 31.5 us
  Pallas kernels: 24.8 us -> 22 us
  local copies, waits for them, and re-layouts: 2.65 us -> 1.21 us
    ppermute x11 -> x13, waiting for transfers between devices: 23.1 us -> 11.6 us  [shifted(): return lax.ppermute(x, axis, [(i, (i + step) % size) for i in range(size)])]
    ppermute x1 -> x2, starting transfers between devices: 5.11 us -> 8.76 us  [local(): twins.append(lax.ppermute(part, 'col', [(i, i ^ 1) for i in range(GRID)]))]
    ppermute x11 -> x13, starting transfers between devices: 19.4 us -> 22.8 us  [shifted(): return lax.ppermute(x, axis, [(i, (i + step) % size) for i in range(size)])]
    pallas_call x1, Pallas kernels: 23.2 us -> 20.4 us  [main(): pl.pallas_call(main_body, out_shape=(jax.ShapeDtypeStruct((SIDE, SIDE), F...]
    ppermute x1 -> x2, waiting for transfers between devices: 4.16 us -> 2.15 us  [local(): twins.append(lax.ppermute(part, 'col', [(i, i ^ 1) for i in range(GRID)]))]
    unnamed x14 -> x12, local copies, waits for them, and re-layouts: 2.57 us -> 1.14 us
  transfers between devices with their start and end apart: 12 -> 15, of which waited for: 5 -> 4; matrix products, arithmetic and copies ran while one was open for 1% -> 2% of each run, Pallas kernels for 0% -> 0%
where the time goes in v3:
time: 70 us; the launch traced here: 69.8 us
  starting transfers between devices  31.5 us (45%)
  Pallas kernels  22 us (31%)
  waiting for transfers between devices  13.8 us (20%)
  local copies, waits for them, and re-layouts  1.21 us (2%)
  between operations  0.93 us (1%)
    ppermute x13, starting transfers between devices, shifted(): return lax.ppermute(x, axis, [(i, (i + step) % size) for i in range(size)])  22.8 us
    pallas_call x1, Pallas kernels, main(): pl.pallas_call(main_body, out_shape=(jax.ShapeDtypeStruct((SIDE, SIDE), F...  20.4 us
    ppermute x13, waiting for transfers between devices, shifted(): return lax.ppermute(x, axis, [(i, (i + step) % size) for i in range(size)])  11.6 us
    ppermute x2, starting transfers between devices, local(): twins.append(lax.ppermute(part, 'col', [(i, i ^ 1) for i in range(GRID)]))  8.76 us
    ppermute x2, waiting for transfers between devices, local(): twins.append(lax.ppermute(part, 'col', [(i, i ^ 1) for i in range(GRID)]))  2.15 us
    pallas_call x1, Pallas kernels, prep(): pl.pallas_call(prep_body, out_shape=jax.ShapeDtypeStruct((ROWS, SIDE), BF...  1.65 us
  transfers between devices with their start and end apart: 15, of which 4 were waited for; matrix products, arithmetic and copies ran while one was open for 2% of the time, Pallas kernels for 0%

profile of v3, /device:TPU:1, one launch (start us, length us, event | category | flops | bytes accessed | tf_op | source)
XLA Modules:
  0.0 69.8 jit_solution(5970939747489212481)
XLA Ops:
  0.6 1.7 %shard_map.49 = bf16[144,256]{1,0:T(8,128)(2,1)} custom-call(f32[256,256]{1,0:T(8,128)} %s_ref.1), custom_call_target="tpu_custom_call" | custom-call | tf_op jit(solution)/shard_map/pallas_call | solution.py:58
  2.3 2.5 %collective-permute-start = (bf16[144,256]{1,0:T(8,128)(2,1)}, bf16[144,256]{1,0:T(8,128)(2,1)S(1)}, u32[]{:S(2)}, u32[]{:S(2)}) collective-permute-start(bf16[144,256]{1,0:T(8,128)(2,1)} %shard_map.49), channel_id=1, source_target_pairs={{0,8},{8,16},{16,24},{24,32},{32,40},{40,48},{48,56},{56,0},{1,9},... | collective-permute-start | bytes 221192 | tf_op jit(solution)/shard_map/ppermute | solution.py:275
  4.8 4.0 %collective-permute-start.1 = (bf16[144,256]{1,0:T(8,128)(2,1)}, bf16[144,256]{1,0:T(8,128)(2,1)S(1)}, u32[]{:S(2)}, u32[]{:S(2)}) collective-permute-start(bf16[144,256]{1,0:T(8,128)(2,1)} %shard_map.49), channel_id=1, source_target_pairs={{0,56},{8,0},{16,8},{24,16},{32,24},{40,32},{48,40},{56,48},{1,57}... | collective-permute-start | bytes 221192 | tf_op jit(solution)/shard_map/ppermute | solution.py:275
  8.8 0.0 collective-permute-start.2
  8.8 3.6 %collective-permute-start.3 = (bf16[144,256]{1,0:T(8,128)(2,1)}, bf16[144,256]{1,0:T(8,128)(2,1)S(1)}, u32[]{:S(2)}, u32[]{:S(2)}) collective-permute-start(bf16[144,256]{1,0:T(8,128)(2,1)} %shard_map.49), channel_id=1, source_target_pairs={{0,48},{8,56},{16,0},{24,8},{32,16},{40,24},{48,32},{56,40},{1,49}... | collective-permute-start | bytes 221192 | tf_op jit(solution)/shard_map/ppermute | solution.py:275
  12.4 0.9 %bitcast_dynamic-update-slice_fusion.12 = (bf16[18,144,256]{2,1,0:T(8,128)(2,1)S(1)}, bf16[32,144,256]{2,1,0:T(8,128)(2,1)S(1)}, bf16[5,144,256]{2,1,0:T(8,128)(2,1)S(1)}) fusion(bf16[144,256]{1,0:T(8,128)(2,1)} %shard_map.49), kind=kLoop, calls=%fused_computation.15 | loop fusion | bytes 294912
  13.3 0.0 collective-permute-done
  13.3 0.8 %collective-permute-start.4 = (bf16[144,256]{1,0:T(8,128)(2,1)S(1)}, bf16[144,256]{1,0:T(8,128)(2,1)S(1)}, u32[]{:S(2)}, u32[]{:S(2)}) collective-permute-start(bf16[144,256]{1,0:T(8,128)(2,1)S(1)} %collective-permute-done), channel_id=1, source_target_pairs={{0,16},{8,24},{16,32},{24,40},{32,48},{40,56},{48,0},{56,8},{1,17}... | collective-permute-start | bytes 221192 | tf_op jit(solution)/shard_map/ppermute | solution.py:275
  14.1 0.0 collective-permute-done.1
  14.1 2.8 %collective-permute-start.5 = (bf16[144,256]{1,0:T(8,128)(2,1)S(1)}, bf16[144,256]{1,0:T(8,128)(2,1)S(1)}, u32[]{:S(2)}, u32[]{:S(2)}) collective-permute-start(bf16[144,256]{1,0:T(8,128)(2,1)S(1)} %collective-permute-done.1), channel_id=1, source_target_pairs={{0,48},{8,56},{16,0},{24,8},{32,16},{40,24},{48,32},{56,40},{1,49}... | collective-permute-start | bytes 221192 | tf_op jit(solution)/shard_map/ppermute | solution.py:275
  17.0 0.0 collective-permute-done.2
  17.0 0.8 %collective-permute-start.6 = (bf16[144,256]{1,0:T(8,128)(2,1)S(1)}, bf16[144,256]{1,0:T(8,128)(2,1)S(1)}, u32[]{:S(2)}, u32[]{:S(2)}) collective-permute-start(bf16[144,256]{1,0:T(8,128)(2,1)S(1)} %collective-permute-done.2), channel_id=1, source_target_pairs={{0,16},{8,24},{16,32},{24,40},{32,48},{40,56},{48,0},{56,8},{1,17}... | collective-permute-start | bytes 221192 | tf_op jit(solution)/shard_map/ppermute | solution.py:275
  17.8 0.0 collective-permute-done.3
  17.9 1.4 %collective-permute-start.7 = (bf16[5,144,256]{2,1,0:T(8,128)(2,1)S(1)}, bf16[5,144,256]{2,1,0:T(8,128)(2,1)S(1)}, u32[]{:S(2)}, u32[]{:S(2)}) collective-permute-start(bf16[5,144,256]{2,1,0:T(8,128)(2,1)S(1)} %get-tuple-element.21), channel_id=1, source_target_pairs={{0,2},{1,3},{2,4},{3,5},{4,6},{5,7},{6,0},{7,1},{8,10},{9,11},{10,... | collective-permute-start | bytes 1105928 | tf_op jit(solution)/shard_map/ppermute | solution.py:275
  19.2 1.4 %collective-permute-start.8 = (bf16[5,144,256]{2,1,0:T(8,128)(2,1)S(1)}, bf16[5,144,256]{2,1,0:T(8,128)(2,1)S(1)}, u32[]{:S(2)}, u32[]{:S(2)}) collective-permute-start(bf16[5,144,256]{2,1,0:T(8,128)(2,1)S(1)} %get-tuple-element.21), channel_id=1, source_target_pairs={{0,6},{1,7},{2,0},{3,1},{4,2},{5,3},{6,4},{7,5},{8,14},{9,15},{10,... | collective-permute-start | bytes 1105928 | tf_op jit(solution)/shard_map/ppermute | solution.py:275
  20.7 0.0 collective-permute-done.4
  20.7 0.0 collective-permute-done.5
  20.7 1.7 %collective-permute-done.6 = bf16[144,256]{1,0:T(8,128)(2,1)S(1)} collective-permute-done((bf16[144,256]{1,0:T(8,128)(2,1)S(1)}, bf16[144,256]{1,0:T(8,128)(2,1)S(1)}, u32[]{:S(2)}, u32[]{:S(2)}) %collective-permute-start.6) | collective-permute-done | bytes 73760 | tf_op jit(solution)/shard_map/ppermute | solution.py:275
  22.4 2.8 %collective-permute-start.10 = (bf16[3,144,256]{2,1,0:T(8,128)(2,1)S(1)}, bf16[3,144,256]{2,1,0:T(8,128)(2,1)S(1)}, u32[]{:S(2)}, u32[]{:S(2)}) collective-permute-start(bf16[3,144,256]{2,1,0:T(8,128)(2,1)S(1)} %pad_maximum_fusion.2), channel_id=1, source_target_pairs={{0,6},{1,7},{2,0},{3,1},{4,2},{5,3},{6,4},{7,5},{8,14},{9,15},{10,... | collective-permute-start | bytes 663560 | tf_op jit(solution)/shard_map/ppermute | solution.py:275
  25.1 0.0 collective-permute-start.9
  25.2 6.3 %collective-permute-done.10 = bf16[3,144,256]{2,1,0:T(8,128)(2,1)S(1)} collective-permute-done((bf16[3,144,256]{2,1,0:T(8,128)(2,1)S(1)}, bf16[3,144,256]{2,1,0:T(8,128)(2,1)S(1)}, u32[]{:S(2)}, u32[]{:S(2)}) %collective-permute-start.10) | collective-permute-done | bytes 221216 | tf_op jit(solution)/shard_map/ppermute | solution.py:275
  31.5 2.7 %collective-permute-start.12 = (bf16[3,144,256]{2,1,0:T(8,128)(2,1)S(1)}, bf16[3,144,256]{2,1,0:T(8,128)(2,1)S(1)}, u32[]{:S(2)}, u32[]{:S(2)}) collective-permute-start(bf16[3,144,256]{2,1,0:T(8,128)(2,1)S(1)} %collective-permute-done.10), channel_id=1, source_target_pairs={{0,6},{1,7},{2,0},{3,1},{4,2},{5,3},{6,4},{7,5},{8,14},{9,15},{10,... | collective-permute-start | bytes 663560 | tf_op jit(solution)/shard_map/ppermute | solution.py:275
  34.2 0.0 collective-permute-done.7
  34.2 0.0 collective-permute-start.11
  34.2 0.0 collective-permute-done.8
  34.3 0.1 constant_dynamic-update-slice_fusion.9
  34.3 3.8 %collective-permute-start.13 = (bf16[18,144,256]{2,1,0:T(8,128)(2,1)S(1)}, bf16[18,144,256]{2,1,0:T(8,128)(2,1)S(1)}, u32[]{:S(2)}, u32[]{:S(2)}) collective-permute-start(bf16[18,144,256]{2,1,0:T(8,128)(2,1)S(1)} %get-tuple-element.9), channel_id=1, source_target_pairs={{0,1},{1,0},{2,3},{3,2},{4,5},{5,4},{6,7},{7,6},{8,9},{9,8},{10,11... | collective-permute-start | bytes 3981320 | tf_op jit(solution)/shard_map/ppermute | solution.py:297
  38.1 0.0 collective-permute-done.9
  38.1 0.0 collective-permute-done.12
  38.1 3.6 %collective-permute-done.11 = bf16[5,144,256]{2,1,0:T(8,128)(2,1)S(1)} collective-permute-done((bf16[5,144,256]{2,1,0:T(8,128)(2,1)S(1)}, bf16[5,144,256]{2,1,0:T(8,128)(2,1)S(1)}, u32[]{:S(2)}, u32[]{:S(2)}) %collective-permute-start.11) | collective-permute-done | bytes 368672 | tf_op jit(solution)/shard_map/ppermute | solution.py:275
  41.8 0.1 pad_maximum_fusion.1
  41.9 5.0 %collective-permute-start.14 = (bf16[14,144,256]{2,1,0:T(8,128)(2,1)S(1)}, bf16[14,144,256]{2,1,0:T(8,128)(2,1)S(1)}, u32[]{:S(2)}, u32[]{:S(2)}) collective-permute-start(bf16[14,144,256]{2,1,0:T(8,128)(2,1)S(1)} %pad_maximum_fusion.1), channel_id=1, source_target_pairs={{0,1},{1,0},{2,3},{3,2},{4,5},{5,4},{6,7},{7,6},{8,9},{9,8},{10,11... | collective-permute-start | bytes 3096584 | tf_op jit(solution)/shard_map/ppermute | solution.py:297
  46.9 0.0 collective-permute-done.13
  47.0 2.2 %collective-permute-done.14 = bf16[14,144,256]{2,1,0:T(8,128)(2,1)S(1)} collective-permute-done((bf16[14,144,256]{2,1,0:T(8,128)(2,1)S(1)}, bf16[14,144,256]{2,1,0:T(8,128)(2,1)S(1)}, u32[]{:S(2)}, u32[]{:S(2)}) %collective-permute-start.14) | collective-permute-done | bytes 1032224 | tf_op jit(solution)/shard_map/ppermute | solution.py:297
  49.1 0.2 pad_maximum_fusion.twin_ref
  49.3 20.4 %shard_map.50 = (f32[256,256]{1,0:T(8,128)}, bf16[448,2048]{1,0:T(8,128)(2,1)}, f32[1,256]{1,0:T(1,128)}) custom-call(bf16[32,144,256]{2,1,0:T(8,128)(2,1)S(1)} %constant_dynamic-update-slice_fusion.own_ref, bf16[32,144,256]{2,1,0:T(8,128)(2,1)S(1)} %pad_maximum_fusion.twin_ref, bf16[448,2048]{1,0:T(8,128)(2,1)} %bitcast.32), custom_call_target="tpu_custom_call" | custom-call | tf_op jit(solution)/shard_map/pallas_call | solution.py:242
  (13 shorter events, 0.3 us)
Async XLA Ops:
  2.3 11.0 %collective-permute-start = (bf16[144,256]{1,0:T(8,128)(2,1)}, bf16[144,256]{1,0:T(8,128)(2,1)S(1)}, u32[]{:S(2)}, u32[]{:S(2)}) collective-permute-start(bf16[144,256]{1,0:T(8,128)(2,1)} %shard_map.49), channel_id=1, source_target_pairs={{0,8},{8,16},{16,24},{24,32},{32,40},{40,48},{48,56},{56,0},{1,9},... | collective-permute-start | bytes 221192 | tf_op jit(solution)/shard_map/ppermute | solution.py:275
  4.8 9.4 %collective-permute-start.1 = (bf16[144,256]{1,0:T(8,128)(2,1)}, bf16[144,256]{1,0:T(8,128)(2,1)S(1)}, u32[]{:S(2)}, u32[]{:S(2)}) collective-permute-start(bf16[144,256]{1,0:T(8,128)(2,1)} %shard_map.49), channel_id=1, source_target_pairs={{0,56},{8,0},{16,8},{24,16},{32,24},{40,32},{48,40},{56,48},{1,57}... | collective-permute-start | bytes 221192 | tf_op jit(solution)/shard_map/ppermute | solution.py:275
  8.8 8.2 %collective-permute-start.2 = (bf16[144,256]{1,0:T(8,128)(2,1)}, bf16[144,256]{1,0:T(8,128)(2,1)S(1)}, u32[]{:S(2)}, u32[]{:S(2)}) collective-permute-start(bf16[144,256]{1,0:T(8,128)(2,1)} %shard_map.49), channel_id=1, source_target_pairs={{0,16},{8,24},{16,32},{24,40},{32,48},{40,56},{48,0},{56,8},{1,17}... | collective-permute-start | bytes 221192 | tf_op jit(solution)/shard_map/ppermute | solution.py:275
  8.8 9.0 %collective-permute-start.3 = (bf16[144,256]{1,0:T(8,128)(2,1)}, bf16[144,256]{1,0:T(8,128)(2,1)S(1)}, u32[]{:S(2)}, u32[]{:S(2)}) collective-permute-start(bf16[144,256]{1,0:T(8,128)(2,1)} %shard_map.49), channel_id=1, source_target_pairs={{0,48},{8,56},{16,0},{24,8},{32,16},{40,24},{48,32},{56,40},{1,49}... | collective-permute-start | bytes 221192 | tf_op jit(solution)/shard_map/ppermute | solution.py:275
  13.3 7.4 %collective-permute-start.4 = (bf16[144,256]{1,0:T(8,128)(2,1)S(1)}, bf16[144,256]{1,0:T(8,128)(2,1)S(1)}, u32[]{:S(2)}, u32[]{:S(2)}) collective-permute-start(bf16[144,256]{1,0:T(8,128)(2,1)S(1)} %collective-permute-done), channel_id=1, source_target_pairs={{0,16},{8,24},{16,32},{24,40},{32,48},{40,56},{48,0},{56,8},{1,17}... | collective-permute-start | bytes 221192 | tf_op jit(solution)/shard_map/ppermute | solution.py:275
  14.1 6.5 %collective-permute-start.5 = (bf16[144,256]{1,0:T(8,128)(2,1)S(1)}, bf16[144,256]{1,0:T(8,128)(2,1)S(1)}, u32[]{:S(2)}, u32[]{:S(2)}) collective-permute-start(bf16[144,256]{1,0:T(8,128)(2,1)S(1)} %collective-permute-done.1), channel_id=1, source_target_pairs={{0,48},{8,56},{16,0},{24,8},{32,16},{40,24},{48,32},{56,40},{1,49}... | collective-permute-start | bytes 221192 | tf_op jit(solution)/shard_map/ppermute | solution.py:275
  17.0 5.4 %collective-permute-start.6 = (bf16[144,256]{1,0:T(8,128)(2,1)S(1)}, bf16[144,256]{1,0:T(8,128)(2,1)S(1)}, u32[]{:S(2)}, u32[]{:S(2)}) collective-permute-start(bf16[144,256]{1,0:T(8,128)(2,1)S(1)} %collective-permute-done.2), channel_id=1, source_target_pairs={{0,16},{8,24},{16,32},{24,40},{32,48},{40,56},{48,0},{56,8},{1,17}... | collective-permute-start | bytes 221192 | tf_op jit(solution)/shard_map/ppermute | solution.py:275
  17.9 16.3 %collective-permute-start.7 = (bf16[5,144,256]{2,1,0:T(8,128)(2,1)S(1)}, bf16[5,144,256]{2,1,0:T(8,128)(2,1)S(1)}, u32[]{:S(2)}, u32[]{:S(2)}) collective-permute-start(bf16[5,144,256]{2,1,0:T(8,128)(2,1)S(1)} %get-tuple-element.21), channel_id=1, source_target_pairs={{0,2},{1,3},{2,4},{3,5},{4,6},{5,7},{6,0},{7,1},{8,10},{9,11},{10,... | collective-permute-start | bytes 1105928 | tf_op jit(solution)/shard_map/ppermute | solution.py:275
  19.2 15.0 %collective-permute-start.8 = (bf16[5,144,256]{2,1,0:T(8,128)(2,1)S(1)}, bf16[5,144,256]{2,1,0:T(8,128)(2,1)S(1)}, u32[]{:S(2)}, u32[]{:S(2)}) collective-permute-start(bf16[5,144,256]{2,1,0:T(8,128)(2,1)S(1)} %get-tuple-element.21), channel_id=1, source_target_pairs={{0,6},{1,7},{2,0},{3,1},{4,2},{5,3},{6,4},{7,5},{8,14},{9,15},{10,... | collective-permute-start | bytes 1105928 | tf_op jit(solution)/shard_map/ppermute | solution.py:275
  22.4 9.1 %collective-permute-start.10 = (bf16[3,144,256]{2,1,0:T(8,128)(2,1)S(1)}, bf16[3,144,256]{2,1,0:T(8,128)(2,1)S(1)}, u32[]{:S(2)}, u32[]{:S(2)}) collective-permute-start(bf16[3,144,256]{2,1,0:T(8,128)(2,1)S(1)} %pad_maximum_fusion.2), channel_id=1, source_target_pairs={{0,6},{1,7},{2,0},{3,1},{4,2},{5,3},{6,4},{7,5},{8,14},{9,15},{10,... | collective-permute-start | bytes 663560 | tf_op jit(solution)/shard_map/ppermute | solution.py:275
  25.1 13.0 %collective-permute-start.9 = (bf16[3,144,256]{2,1,0:T(8,128)(2,1)S(1)}, bf16[3,144,256]{2,1,0:T(8,128)(2,1)S(1)}, u32[]{:S(2)}, u32[]{:S(2)}) collective-permute-start(bf16[3,144,256]{2,1,0:T(8,128)(2,1)S(1)} %pad_maximum_fusion.2), channel_id=1, source_target_pairs={{0,2},{1,3},{2,4},{3,5},{4,6},{5,7},{6,0},{7,1},{8,10},{9,11},{10,... | collective-permute-start | bytes 663560 | tf_op jit(solution)/shard_map/ppermute | solution.py:275
  31.5 6.6 %collective-permute-start.12 = (bf16[3,144,256]{2,1,0:T(8,128)(2,1)S(1)}, bf16[3,144,256]{2,1,0:T(8,128)(2,1)S(1)}, u32[]{:S(2)}, u32[]{:S(2)}) collective-permute-start(bf16[3,144,256]{2,1,0:T(8,128)(2,1)S(1)} %collective-permute-done.10), channel_id=1, source_target_pairs={{0,6},{1,7},{2,0},{3,1},{4,2},{5,3},{6,4},{7,5},{8,14},{9,15},{10,... | collective-permute-start | bytes 663560 | tf_op jit(solution)/shard_map/ppermute | solution.py:275
  34.2 7.6 %collective-permute-start.11 = (bf16[5,144,256]{2,1,0:T(8,128)(2,1)S(1)}, bf16[5,144,256]{2,1,0:T(8,128)(2,1)S(1)}, u32[]{:S(2)}, u32[]{:S(2)}) collective-permute-start(bf16[5,144,256]{2,1,0:T(8,128)(2,1)S(1)} %collective-permute-done.7), channel_id=1, source_target_pairs={{0,2},{1,3},{2,4},{3,5},{4,6},{5,7},{6,0},{7,1},{8,10},{9,11},{10,... | collective-permute-start | bytes 1105928 | tf_op jit(solution)/shard_map/ppermute | solution.py:275
  34.3 12.6 %collective-permute-start.13 = (bf16[18,144,256]{2,1,0:T(8,128)(2,1)S(1)}, bf16[18,144,256]{2,1,0:T(8,128)(2,1)S(1)}, u32[]{:S(2)}, u32[]{:S(2)}) collective-permute-start(bf16[18,144,256]{2,1,0:T(8,128)(2,1)S(1)} %get-tuple-element.9), channel_id=1, source_target_pairs={{0,1},{1,0},{2,3},{3,2},{4,5},{5,4},{6,7},{7,6},{8,9},{9,8},{10,11... | collective-permute-start | bytes 3981320 | tf_op jit(solution)/shard_map/ppermute | solution.py:297
  41.9 7.2 %collective-permute-start.14 = (bf16[14,144,256]{2,1,0:T(8,128)(2,1)S(1)}, bf16[14,144,256]{2,1,0:T(8,128)(2,1)S(1)}, u32[]{:S(2)}, u32[]{:S(2)}) collective-permute-start(bf16[14,144,256]{2,1,0:T(8,128)(2,1)S(1)} %pad_maximum_fusion.1), channel_id=1, source_target_pairs={{0,1},{1,0},{2,3},{3,2},{4,5},{5,4},{6,7},{7,6},{8,9},{9,8},{10,11... | collective-permute-start | bytes 3096584 | tf_op jit(solution)/shard_map/ppermute | solution.py:297

commit v4 on v3

--- a/solution.py
+++ b/solution.py
@@ -67,7 +67,7 @@
     return pl.ds(pl.multiple_of(index * size, size), size)
 
 
-TILE = 512
+TILE = 1024
 
 
 def main_body(own_ref, twin_ref, g_hbm, m_ref, pre_hbm, nd_ref, g_ref, pre_ref,
@@ -179,7 +179,7 @@
         leave(n).start()
         return 0
 
-    lax.fori_loop(0, BLOCK // TILE, spread, 0)
+    lax.fori_loop(0, BLOCK // TILE, spread, 0, unroll=True)
 
     v_ref[:, :SIDE] = o_ref[:, block_of(SIDE, row)]
     v_ref[:, SIDE:] = o_ref[:, block_of(SIDE, col)]
@@ -195,7 +195,7 @@
         th_ref[rows, :] = t.astype(BF16)
         return 0
 
-    lax.fori_loop(0, BLOCK // TILE, two, 0)
+    lax.fori_loop(0, BLOCK // TILE, two, 0, unroll=True)
 
     ones = d_cols * inv
     alone = (25.0 - 10.0 * ones + ones * ones) * 0.0625
@@ -219,7 +219,7 @@
         ob_ref[rows, :] = third[:, SIDE:].astype(BF16)
         return acc + jnp.sum(t[:, :SIDE] * third[:, :SIDE], axis=0, keepdims=True)
 
-    nd_ref[...] = lax.fori_loop(0, BLOCK // TILE, three, jnp.zeros((1, SIDE), F32))
+    nd_ref[...] = lax.fori_loop(0, BLOCK // TILE, three, jnp.zeros((1, SIDE), F32), unroll=True)
 
     rows = block_of(SIDE, col)
     third = third_ref[rows, :]
@@ -284,7 +284,8 @@
     up4 = shifted(up2, "row", 2)
     rest = jnp.stack([up3, down3, up4])
     rest_over, rest_under = shifted(rest, "col", 2), shifted(rest, "col", -2)
-    far = [shifted(near_over, "col", 2), shifted(rest_under, "col", -2)]
+    back = jnp.concatenate([near_under[4:], rest_under])
+    far = [shifted(near_over[:4], "col", 2), shifted(back, "col", -2)]
     early = jnp.concatenate([near, rest, near_over, near_under])
     late = jnp.concatenate([rest_over, rest_under, *far])
     return early, late

time: 70 us -> 64.4 us (0.920)
  waiting for transfers between devices: 13.8 us -> 9.87 us
  Pallas kernels: 22 us -> 20.4 us
    ppermute x13, waiting for transfers between devices: 11.6 us -> 7.7 us  [shifted(): return lax.ppermute(x, axis, [(i, (i + step) % size) for i in range(size)])]
    pallas_call x1, Pallas kernels: 20.4 us -> 18.8 us  [main(): pl.pallas_call(main_body, out_shape=(jax.ShapeDtypeStruct((SIDE, SIDE), F...]
    ppermute x2, starting transfers between devices: 8.76 us -> 7.92 us  [local(): twins.append(lax.ppermute(part, 'col', [(i, i ^ 1) for i in range(GRID)]))]
where the time goes in v4:
time: 64.4 us; the launch traced here: 63.9 us
  starting transfers between devices  31 us (48%)
  Pallas kernels  20.4 us (32%)
  waiting for transfers between devices  9.87 us (15%)
  local copies, waits for them, and re-layouts  1.24 us (2%)
  between operations  0.94 us (1%)
    ppermute x13, starting transfers between devices, shifted(): return lax.ppermute(x, axis, [(i, (i + step) % size) for i in range(size)])  23.1 us
    pallas_call x1, Pallas kernels, main(): pl.pallas_call(main_body, out_shape=(jax.ShapeDtypeStruct((SIDE, SIDE), F...  18.8 us
    ppermute x2, starting transfers between devices, local(): twins.append(lax.ppermute(part, 'col', [(i, i ^ 1) for i in range(GRID)]))  7.92 us
    ppermute x13, waiting for transfers between devices, shifted(): return lax.ppermute(x, axis, [(i, (i + step) % size) for i in range(size)])  7.7 us
    ppermute x2, waiting for transfers between devices, local(): twins.append(lax.ppermute(part, 'col', [(i, i ^ 1) for i in range(GRID)]))  2.16 us
    pallas_call x1, Pallas kernels, prep(): pl.pallas_call(prep_body, out_shape=jax.ShapeDtypeStruct((ROWS, SIDE), BF...  1.65 us
  transfers between devices with their start and end apart: 15, of which 4 were waited for; matrix products, arithmetic and copies ran while one was open for 2% of the time, Pallas kernels for 0%

profile of v4, /device:TPU:1, one launch (start us, length us, event | category | flops | bytes accessed | tf_op | source)
XLA Modules:
  0.0 63.9 jit_solution(2454228896507626958)
XLA Ops:
  0.6 1.7 %shard_map.49 = bf16[144,256]{1,0:T(8,128)(2,1)} custom-call(f32[256,256]{1,0:T(8,128)} %s_ref.1), custom_call_target="tpu_custom_call" | custom-call | tf_op jit(solution)/shard_map/pallas_call | solution.py:58
  2.3 2.5 %collective-permute-start = (bf16[144,256]{1,0:T(8,128)(2,1)}, bf16[144,256]{1,0:T(8,128)(2,1)S(1)}, u32[]{:S(2)}, u32[]{:S(2)}) collective-permute-start(bf16[144,256]{1,0:T(8,128)(2,1)} %shard_map.49), channel_id=1, source_target_pairs={{0,8},{8,16},{16,24},{24,32},{32,40},{40,48},{48,56},{56,0},{1,9},... | collective-permute-start | bytes 221192 | tf_op jit(solution)/shard_map/ppermute | solution.py:275
  4.8 4.0 %collective-permute-start.1 = (bf16[144,256]{1,0:T(8,128)(2,1)}, bf16[144,256]{1,0:T(8,128)(2,1)S(1)}, u32[]{:S(2)}, u32[]{:S(2)}) collective-permute-start(bf16[144,256]{1,0:T(8,128)(2,1)} %shard_map.49), channel_id=1, source_target_pairs={{0,56},{8,0},{16,8},{24,16},{32,24},{40,32},{48,40},{56,48},{1,57}... | collective-permute-start | bytes 221192 | tf_op jit(solution)/shard_map/ppermute | solution.py:275
  8.8 0.0 collective-permute-start.2
  8.8 3.6 %collective-permute-start.3 = (bf16[144,256]{1,0:T(8,128)(2,1)}, bf16[144,256]{1,0:T(8,128)(2,1)S(1)}, u32[]{:S(2)}, u32[]{:S(2)}) collective-permute-start(bf16[144,256]{1,0:T(8,128)(2,1)} %shard_map.49), channel_id=1, source_target_pairs={{0,48},{8,56},{16,0},{24,8},{32,16},{40,24},{48,32},{56,40},{1,49}... | collective-permute-start | bytes 221192 | tf_op jit(solution)/shard_map/ppermute | solution.py:275
  12.4 0.9 %bitcast_dynamic-update-slice_fusion.12 = (bf16[18,144,256]{2,1,0:T(8,128)(2,1)S(1)}, bf16[32,144,256]{2,1,0:T(8,128)(2,1)S(1)}, bf16[5,144,256]{2,1,0:T(8,128)(2,1)S(1)}) fusion(bf16[144,256]{1,0:T(8,128)(2,1)} %shard_map.49), kind=kLoop, calls=%fused_computation.16 | loop fusion | bytes 294912
  13.3 0.0 collective-permute-done
  13.3 0.8 %collective-permute-start.4 = (bf16[144,256]{1,0:T(8,128)(2,1)S(1)}, bf16[144,256]{1,0:T(8,128)(2,1)S(1)}, u32[]{:S(2)}, u32[]{:S(2)}) collective-permute-start(bf16[144,256]{1,0:T(8,128)(2,1)S(1)} %collective-permute-done), channel_id=1, source_target_pairs={{0,16},{8,24},{16,32},{24,40},{32,48},{40,56},{48,0},{56,8},{1,17}... | collective-permute-start | bytes 221192 | tf_op jit(solution)/shard_map/ppermute | solution.py:275
  14.1 0.0 collective-permute-done.1
  14.1 2.8 %collective-permute-start.5 = (bf16[144,256]{1,0:T(8,128)(2,1)S(1)}, bf16[144,256]{1,0:T(8,128)(2,1)S(1)}, u32[]{:S(2)}, u32[]{:S(2)}) collective-permute-start(bf16[144,256]{1,0:T(8,128)(2,1)S(1)} %collective-permute-done.1), channel_id=1, source_target_pairs={{0,48},{8,56},{16,0},{24,8},{32,16},{40,24},{48,32},{56,40},{1,49}... | collective-permute-start | bytes 221192 | tf_op jit(solution)/shard_map/ppermute | solution.py:275
  17.0 0.0 collective-permute-done.2
  17.0 0.8 %collective-permute-start.6 = (bf16[144,256]{1,0:T(8,128)(2,1)S(1)}, bf16[144,256]{1,0:T(8,128)(2,1)S(1)}, u32[]{:S(2)}, u32[]{:S(2)}) collective-permute-start(bf16[144,256]{1,0:T(8,128)(2,1)S(1)} %collective-permute-done.2), channel_id=1, source_target_pairs={{0,16},{8,24},{16,32},{24,40},{32,48},{40,56},{48,0},{56,8},{1,17}... | collective-permute-start | bytes 221192 | tf_op jit(solution)/shard_map/ppermute | solution.py:275
  17.8 0.0 collective-permute-done.3
  17.9 1.4 %collective-permute-start.7 = (bf16[5,144,256]{2,1,0:T(8,128)(2,1)S(1)}, bf16[5,144,256]{2,1,0:T(8,128)(2,1)S(1)}, u32[]{:S(2)}, u32[]{:S(2)}) collective-permute-start(bf16[5,144,256]{2,1,0:T(8,128)(2,1)S(1)} %get-tuple-element.21), channel_id=1, source_target_pairs={{0,2},{1,3},{2,4},{3,5},{4,6},{5,7},{6,0},{7,1},{8,10},{9,11},{10,... | collective-permute-start | bytes 1105928 | tf_op jit(solution)/shard_map/ppermute | solution.py:275
  19.2 1.4 %collective-permute-start.8 = (bf16[5,144,256]{2,1,0:T(8,128)(2,1)S(1)}, bf16[5,144,256]{2,1,0:T(8,128)(2,1)S(1)}, u32[]{:S(2)}, u32[]{:S(2)}) collective-permute-start(bf16[5,144,256]{2,1,0:T(8,128)(2,1)S(1)} %get-tuple-element.21), channel_id=1, source_target_pairs={{0,6},{1,7},{2,0},{3,1},{4,2},{5,3},{6,4},{7,5},{8,14},{9,15},{10,... | collective-permute-start | bytes 1105928 | tf_op jit(solution)/shard_map/ppermute | solution.py:275
  20.7 0.0 collective-permute-done.4
  20.7 0.0 collective-permute-done.5
  20.7 1.7 %collective-permute-done.6 = bf16[144,256]{1,0:T(8,128)(2,1)S(1)} collective-permute-done((bf16[144,256]{1,0:T(8,128)(2,1)S(1)}, bf16[144,256]{1,0:T(8,128)(2,1)S(1)}, u32[]{:S(2)}, u32[]{:S(2)}) %collective-permute-start.6) | collective-permute-done | bytes 73760 | tf_op jit(solution)/shard_map/ppermute | solution.py:275
  22.4 1.4 %collective-permute-start.9 = (bf16[3,144,256]{2,1,0:T(8,128)(2,1)S(1)}, bf16[3,144,256]{2,1,0:T(8,128)(2,1)S(1)}, u32[]{:S(2)}, u32[]{:S(2)}) collective-permute-start(bf16[3,144,256]{2,1,0:T(8,128)(2,1)S(1)} %pad_maximum_fusion.3), channel_id=1, source_target_pairs={{0,2},{1,3},{2,4},{3,5},{4,6},{5,7},{6,0},{7,1},{8,10},{9,11},{10,... | collective-permute-start | bytes 663560 | tf_op jit(solution)/shard_map/ppermute | solution.py:275
  23.8 1.5 %collective-permute-start.10 = (bf16[3,144,256]{2,1,0:T(8,128)(2,1)S(1)}, bf16[3,144,256]{2,1,0:T(8,128)(2,1)S(1)}, u32[]{:S(2)}, u32[]{:S(2)}) collective-permute-start(bf16[3,144,256]{2,1,0:T(8,128)(2,1)S(1)} %pad_maximum_fusion.3), channel_id=1, source_target_pairs={{0,6},{1,7},{2,0},{3,1},{4,2},{5,3},{6,4},{7,5},{8,14},{9,15},{10,... | collective-permute-start | bytes 663560 | tf_op jit(solution)/shard_map/ppermute | solution.py:275
  25.3 1.6 %collective-permute-done.7 = bf16[5,144,256]{2,1,0:T(8,128)(2,1)S(1)} collective-permute-done((bf16[5,144,256]{2,1,0:T(8,128)(2,1)S(1)}, bf16[5,144,256]{2,1,0:T(8,128)(2,1)S(1)}, u32[]{:S(2)}, u32[]{:S(2)}) %collective-permute-start.7) | collective-permute-done | bytes 368672 | tf_op jit(solution)/shard_map/ppermute | solution.py:275
  27.0 0.2 collective-permute-start.11
  27.1 0.0 collective-permute-done.8
  27.1 4.3 %collective-permute-done.10 = bf16[3,144,256]{2,1,0:T(8,128)(2,1)S(1)} collective-permute-done((bf16[3,144,256]{2,1,0:T(8,128)(2,1)S(1)}, bf16[3,144,256]{2,1,0:T(8,128)(2,1)S(1)}, u32[]{:S(2)}, u32[]{:S(2)}) %collective-permute-start.10) | collective-permute-done | bytes 221216 | tf_op jit(solution)/shard_map/ppermute | solution.py:275
  31.5 2.8 %collective-permute-start.12 = (bf16[4,144,256]{2,1,0:T(8,128)(2,1)S(1)}, bf16[4,144,256]{2,1,0:T(8,128)(2,1)S(1)}, u32[]{:S(2)}, u32[]{:S(2)}) collective-permute-start(bf16[4,144,256]{2,1,0:T(8,128)(2,1)S(1)} %pad_maximum_fusion.2), channel_id=1, source_target_pairs={{0,6},{1,7},{2,0},{3,1},{4,2},{5,3},{6,4},{7,5},{8,14},{9,15},{10,... | collective-permute-start | bytes 884744 | tf_op jit(solution)/shard_map/ppermute | solution.py:275
  34.3 0.1 constant_dynamic-update-slice_fusion.9
  34.4 3.8 %collective-permute-start.13 = (bf16[18,144,256]{2,1,0:T(8,128)(2,1)S(1)}, bf16[18,144,256]{2,1,0:T(8,128)(2,1)S(1)}, u32[]{:S(2)}, u32[]{:S(2)}) collective-permute-start(bf16[18,144,256]{2,1,0:T(8,128)(2,1)S(1)} %get-tuple-element.9), channel_id=1, source_target_pairs={{0,1},{1,0},{2,3},{3,2},{4,5},{5,4},{6,7},{7,6},{8,9},{9,8},{10,11... | collective-permute-start | bytes 3981320 | tf_op jit(solution)/shard_map/ppermute | solution.py:298
  38.2 0.0 collective-permute-done.9
  38.2 0.0 collective-permute-done.11
  38.2 0.0 collective-permute-done.12
  38.2 0.1 pad_maximum_fusion.1
  38.4 4.1 %collective-permute-start.14 = (bf16[14,144,256]{2,1,0:T(8,128)(2,1)S(1)}, bf16[14,144,256]{2,1,0:T(8,128)(2,1)S(1)}, u32[]{:S(2)}, u32[]{:S(2)}) collective-permute-start(bf16[14,144,256]{2,1,0:T(8,128)(2,1)S(1)} %pad_maximum_fusion.1), channel_id=1, source_target_pairs={{0,1},{1,0},{2,3},{3,2},{4,5},{5,4},{6,7},{7,6},{8,9},{9,8},{10,11... | collective-permute-start | bytes 3096584 | tf_op jit(solution)/shard_map/ppermute | solution.py:298
  42.6 2.2 %collective-permute-done.14 = bf16[14,144,256]{2,1,0:T(8,128)(2,1)S(1)} collective-permute-done((bf16[14,144,256]{2,1,0:T(8,128)(2,1)S(1)}, bf16[14,144,256]{2,1,0:T(8,128)(2,1)S(1)}, u32[]{:S(2)}, u32[]{:S(2)}) %collective-permute-start.14) | collective-permute-done | bytes 1032224 | tf_op jit(solution)/shard_map/ppermute | solution.py:298
  44.7 0.0 collective-permute-done.13
  44.7 0.2 pad_maximum_fusion.twin_ref
  44.9 18.8 %shard_map.50 = (f32[256,256]{1,0:T(8,128)}, bf16[448,2048]{1,0:T(8,128)(2,1)}, f32[1,256]{1,0:T(1,128)}) custom-call(bf16[32,144,256]{2,1,0:T(8,128)(2,1)S(1)} %constant_dynamic-update-slice_fusion.own_ref, bf16[32,144,256]{2,1,0:T(8,128)(2,1)S(1)} %pad_maximum_fusion.twin_ref, bf16[448,2048]{1,0:T(8,128)(2,1)} %bitcast.32), custom_call_target="tpu_custom_call" | custom-call | tf_op jit(solution)/shard_map/pallas_call | solution.py:242
  (16 shorter events, 0.3 us)
Async XLA Ops:
  2.3 11.0 %collective-permute-start = (bf16[144,256]{1,0:T(8,128)(2,1)}, bf16[144,256]{1,0:T(8,128)(2,1)S(1)}, u32[]{:S(2)}, u32[]{:S(2)}) collective-permute-start(bf16[144,256]{1,0:T(8,128)(2,1)} %shard_map.49), channel_id=1, source_target_pairs={{0,8},{8,16},{16,24},{24,32},{32,40},{40,48},{48,56},{56,0},{1,9},... | collective-permute-start | bytes 221192 | tf_op jit(solution)/shard_map/ppermute | solution.py:275
  4.8 9.4 %collective-permute-start.1 = (bf16[144,256]{1,0:T(8,128)(2,1)}, bf16[144,256]{1,0:T(8,128)(2,1)S(1)}, u32[]{:S(2)}, u32[]{:S(2)}) collective-permute-start(bf16[144,256]{1,0:T(8,128)(2,1)} %shard_map.49), channel_id=1, source_target_pairs={{0,56},{8,0},{16,8},{24,16},{32,24},{40,32},{48,40},{56,48},{1,57}... | collective-permute-start | bytes 221192 | tf_op jit(solution)/shard_map/ppermute | solution.py:275
  8.8 8.2 %collective-permute-start.2 = (bf16[144,256]{1,0:T(8,128)(2,1)}, bf16[144,256]{1,0:T(8,128)(2,1)S(1)}, u32[]{:S(2)}, u32[]{:S(2)}) collective-permute-start(bf16[144,256]{1,0:T(8,128)(2,1)} %shard_map.49), channel_id=1, source_target_pairs={{0,16},{8,24},{16,32},{24,40},{32,48},{40,56},{48,0},{56,8},{1,17}... | collective-permute-start | bytes 221192 | tf_op jit(solution)/shard_map/ppermute | solution.py:275
  8.8 9.0 %collective-permute-start.3 = (bf16[144,256]{1,0:T(8,128)(2,1)}, bf16[144,256]{1,0:T(8,128)(2,1)S(1)}, u32[]{:S(2)}, u32[]{:S(2)}) collective-permute-start(bf16[144,256]{1,0:T(8,128)(2,1)} %shard_map.49), channel_id=1, source_target_pairs={{0,48},{8,56},{16,0},{24,8},{32,16},{40,24},{48,32},{56,40},{1,49}... | collective-permute-start | bytes 221192 | tf_op jit(solution)/shard_map/ppermute | solution.py:275
  13.3 7.4 %collective-permute-start.4 = (bf16[144,256]{1,0:T(8,128)(2,1)S(1)}, bf16[144,256]{1,0:T(8,128)(2,1)S(1)}, u32[]{:S(2)}, u32[]{:S(2)}) collective-permute-start(bf16[144,256]{1,0:T(8,128)(2,1)S(1)} %collective-permute-done), channel_id=1, source_target_pairs={{0,16},{8,24},{16,32},{24,40},{32,48},{40,56},{48,0},{56,8},{1,17}... | collective-permute-start | bytes 221192 | tf_op jit(solution)/shard_map/ppermute | solution.py:275
  14.1 6.5 %collective-permute-start.5 = (bf16[144,256]{1,0:T(8,128)(2,1)S(1)}, bf16[144,256]{1,0:T(8,128)(2,1)S(1)}, u32[]{:S(2)}, u32[]{:S(2)}) collective-permute-start(bf16[144,256]{1,0:T(8,128)(2,1)S(1)} %collective-permute-done.1), channel_id=1, source_target_pairs={{0,48},{8,56},{16,0},{24,8},{32,16},{40,24},{48,32},{56,40},{1,49}... | collective-permute-start | bytes 221192 | tf_op jit(solution)/shard_map/ppermute | solution.py:275
  17.0 5.4 %collective-permute-start.6 = (bf16[144,256]{1,0:T(8,128)(2,1)S(1)}, bf16[144,256]{1,0:T(8,128)(2,1)S(1)}, u32[]{:S(2)}, u32[]{:S(2)}) collective-permute-start(bf16[144,256]{1,0:T(8,128)(2,1)S(1)} %collective-permute-done.2), channel_id=1, source_target_pairs={{0,16},{8,24},{16,32},{24,40},{32,48},{40,56},{48,0},{56,8},{1,17}... | collective-permute-start | bytes 221192 | tf_op jit(solution)/shard_map/ppermute | solution.py:275
  17.9 9.1 %collective-permute-start.7 = (bf16[5,144,256]{2,1,0:T(8,128)(2,1)S(1)}, bf16[5,144,256]{2,1,0:T(8,128)(2,1)S(1)}, u32[]{:S(2)}, u32[]{:S(2)}) collective-permute-start(bf16[5,144,256]{2,1,0:T(8,128)(2,1)S(1)} %get-tuple-element.21), channel_id=1, source_target_pairs={{0,2},{1,3},{2,4},{3,5},{4,6},{5,7},{6,0},{7,1},{8,10},{9,11},{10,... | collective-permute-start | bytes 1105928 | tf_op jit(solution)/shard_map/ppermute | solution.py:275
  19.2 7.9 %collective-permute-start.8 = (bf16[5,144,256]{2,1,0:T(8,128)(2,1)S(1)}, bf16[5,144,256]{2,1,0:T(8,128)(2,1)S(1)}, u32[]{:S(2)}, u32[]{:S(2)}) collective-permute-start(bf16[5,144,256]{2,1,0:T(8,128)(2,1)S(1)} %get-tuple-element.21), channel_id=1, source_target_pairs={{0,6},{1,7},{2,0},{3,1},{4,2},{5,3},{6,4},{7,5},{8,14},{9,15},{10,... | collective-permute-start | bytes 1105928 | tf_op jit(solution)/shard_map/ppermute | solution.py:275
  22.4 15.8 %collective-permute-start.9 = (bf16[3,144,256]{2,1,0:T(8,128)(2,1)S(1)}, bf16[3,144,256]{2,1,0:T(8,128)(2,1)S(1)}, u32[]{:S(2)}, u32[]{:S(2)}) collective-permute-start(bf16[3,144,256]{2,1,0:T(8,128)(2,1)S(1)} %pad_maximum_fusion.3), channel_id=1, source_target_pairs={{0,2},{1,3},{2,4},{3,5},{4,6},{5,7},{6,0},{7,1},{8,10},{9,11},{10,... | collective-permute-start | bytes 663560 | tf_op jit(solution)/shard_map/ppermute | solution.py:275
  23.8 7.7 %collective-permute-start.10 = (bf16[3,144,256]{2,1,0:T(8,128)(2,1)S(1)}, bf16[3,144,256]{2,1,0:T(8,128)(2,1)S(1)}, u32[]{:S(2)}, u32[]{:S(2)}) collective-permute-start(bf16[3,144,256]{2,1,0:T(8,128)(2,1)S(1)} %pad_maximum_fusion.3), channel_id=1, source_target_pairs={{0,6},{1,7},{2,0},{3,1},{4,2},{5,3},{6,4},{7,5},{8,14},{9,15},{10,... | collective-permute-start | bytes 663560 | tf_op jit(solution)/shard_map/ppermute | solution.py:275
  27.0 11.3 %collective-permute-start.11 = (bf16[4,144,256]{2,1,0:T(8,128)(2,1)S(1)}, bf16[4,144,256]{2,1,0:T(8,128)(2,1)S(1)}, u32[]{:S(2)}, u32[]{:S(2)}) collective-permute-start(bf16[4,144,256]{2,1,0:T(8,128)(2,1)S(1)} %slice.8), channel_id=1, source_target_pairs={{0,2},{1,3},{2,4},{3,5},{4,6},{5,7},{6,0},{7,1},{8,10},{9,11},{10,... | collective-permute-start | bytes 884744 | tf_op jit(solution)/shard_map/ppermute | solution.py:275
  31.5 6.7 %collective-permute-start.12 = (bf16[4,144,256]{2,1,0:T(8,128)(2,1)S(1)}, bf16[4,144,256]{2,1,0:T(8,128)(2,1)S(1)}, u32[]{:S(2)}, u32[]{:S(2)}) collective-permute-start(bf16[4,144,256]{2,1,0:T(8,128)(2,1)S(1)} %pad_maximum_fusion.2), channel_id=1, source_target_pairs={{0,6},{1,7},{2,0},{3,1},{4,2},{5,3},{6,4},{7,5},{8,14},{9,15},{10,... | collective-permute-start | bytes 884744 | tf_op jit(solution)/shard_map/ppermute | solution.py:275
  34.4 10.3 %collective-permute-start.13 = (bf16[18,144,256]{2,1,0:T(8,128)(2,1)S(1)}, bf16[18,144,256]{2,1,0:T(8,128)(2,1)S(1)}, u32[]{:S(2)}, u32[]{:S(2)}) collective-permute-start(bf16[18,144,256]{2,1,0:T(8,128)(2,1)S(1)} %get-tuple-element.9), channel_id=1, source_target_pairs={{0,1},{1,0},{2,3},{3,2},{4,5},{5,4},{6,7},{7,6},{8,9},{9,8},{10,11... | collective-permute-start | bytes 3981320 | tf_op jit(solution)/shard_map/ppermute | solution.py:298
  38.4 6.4 %collective-permute-start.14 = (bf16[14,144,256]{2,1,0:T(8,128)(2,1)S(1)}, bf16[14,144,256]{2,1,0:T(8,128)(2,1)S(1)}, u32[]{:S(2)}, u32[]{:S(2)}) collective-permute-start(bf16[14,144,256]{2,1,0:T(8,128)(2,1)S(1)} %pad_maximum_fusion.1), channel_id=1, source_target_pairs={{0,1},{1,0},{2,3},{3,2},{4,5},{5,4},{6,7},{7,6},{8,9},{9,8},{10,11... | collective-permute-start | bytes 3096584 | tf_op jit(solution)/shard_map/ppermute | solution.py:298
